TPU v7x, 32 devices: a whole 2x2x4 slice. The times are simulated.
32 devices in a mesh: groups: 2 (over y), tensor: 4 (over z), section: 4 (over x, core).
Axes of the slice: x: 2, y: 2, z: 4, core: 2. Of those that a mesh axis runs over, the one named last changes fastest.
Arguments:
- hidden: bfloat16 [16, 8192], P('groups', 'tensor'), parts along dimension 0, may hold values from -6 to 6
- norm_gain: bfloat16 [4, 8192], P('section'), may hold values from 0.5 to 1.5
- query_weight: bfloat16 [4, 8192, 512], P('section', None, 'tensor'), may hold values from -0.0625 to 0.0625
- query_bias: bfloat16 [4, 512], P('section', 'tensor'), may hold values from -10 to 10
- kv_weight: bfloat16 [4, 8192, 1024], P('section', None, 'tensor'), may hold values from -0.0625 to 0.0625
- out_weight: bfloat16 [4, 512, 8192], P('section', None, 'tensor'), may hold values from -0.25 to 0.25
- kv_pool: bfloat16 [4, 48, 16, 1024], P('section', ('groups', 'tensor')), parts along dimension 1, may hold values from -8 to 8
- page_table: int32 [16, 4], P(('groups', 'tensor')), parts along dimension 0, may hold values from 0 to 23, as said below
- context_len: int32 [16], P(('groups', 'tensor')), parts along dimension 0, may hold values from 33 to 64, as said below
Outputs:
- result: bfloat16 [16, 8192], P(('groups', 'section'), 'tensor'), parts along dimension 0
There are 2 independent parts, one for each index of `groups`. A program takes and returns all parts, laid end to end along the dimension named above; an argument that names none is the same for every part. Nothing has to cross between parts.
Inputs may be any that keep to these rules, and one draw needn't show every extreme that they name: `page_table`: sample r belongs to block k = r // 2; its 4 pages lie in k * 6 to (k + 1) * 6 - 1. The first 2 pages are the same for all samples of a block, every other page belongs to one sample only. `context_len`: some sample has 64 cached tokens.
All inputs are finite; a program needn't handle non-finite values.
Results may differ from a plain program's by a relative error of at most 0.018.
Values may be sent and summed in bfloat16 or wider, within the bound.
No kernel may reach another device: no remote copies, remote signals or barrier semaphores. Data moves between devices by JAX's collectives and lax.ppermute only.
A program may use at most 64 MiB of HBM per device.

v0:
```python
import jax
import jax.numpy as jnp
from jax import lax
from jax.sharding import PartitionSpec as P

HD = 128
KVH = 4


epsilon = 1e-06
rope_base = 1000000.0


def shifted(value, axis, steps):
    count = lax.axis_size(axis)
    initial, last = (max(0, -steps), min(count, count - steps))
    return lax.ppermute(value, axis, [(source, source + steps) for source in range(initial, last)])


def rotate(values, position):
    head_size = values.shape[-1]
    half_size = head_size // 2
    frequency = rope_base ** (-(jnp.arange(half_size, dtype=jnp.float32) * 2.0) / head_size)
    angles = position.astype(jnp.float32)[:, None] * frequency[None, :]
    cosine = jnp.cos(angles)[:, None, :]
    sine_part = jnp.sin(angles)[:, None, :]
    front_half = values[..., :half_size]
    back_half = values[..., half_size:]
    return jnp.concatenate(
        [front_half * cosine - back_half * sine_part, back_half * cosine + front_half * sine_part],
        axis=-1,
    )


def attend(queries, key_new, value_new, cached, position):
    row_count, head_count, head_size = queries.shape
    kv_heads = key_new.shape[1]
    group_size = head_count // kv_heads
    span_len = cached.shape[1]
    keys_all = cached[:, :, : kv_heads * head_size].reshape(
        row_count, span_len, kv_heads, head_size
    )
    values_all = cached[:, :, kv_heads * head_size :].reshape(
        row_count, span_len, kv_heads, head_size
    )
    grouped = queries.reshape(row_count, kv_heads, group_size, head_size)
    scaling = head_size ** (-0.5)
    scores = (
        jnp.einsum("rkgd,rskd->rkgs", grouped, keys_all, preferred_element_type=jnp.float32)
        * scaling
    )
    own_score = (
        jnp.einsum("rkgd,rkd->rkg", grouped, key_new, preferred_element_type=jnp.float32) * scaling
    )
    usable = (jnp.arange(span_len, dtype=jnp.int32)[None, :] < position[:, None])[:, None, None, :]
    row_max = jnp.maximum(jnp.max(jnp.where(usable, scores, -1e30), axis=-1), own_score)
    weights = jnp.where(usable, jnp.exp(scores - row_max[..., None]), 0.0)
    own_weight = jnp.exp(own_score - row_max)
    denominator = jnp.sum(weights, axis=-1) + own_weight
    weights = (weights / denominator[..., None]).astype(jnp.bfloat16)
    own_weight = (own_weight / denominator).astype(jnp.bfloat16)
    mixture = jnp.einsum("rkgs,rskd->rkgd", weights, values_all, preferred_element_type=jnp.float32)
    mixture = (
        mixture
        + own_weight.astype(jnp.float32)[..., None] * value_new.astype(jnp.float32)[:, :, None, :]
    )
    return mixture.reshape(row_count, head_count * head_size).astype(jnp.bfloat16)


def shards(
    hidden,
    norm_gain,
    query_weight,
    query_bias,
    kv_weight,
    out_weight,
    kv_pool,
    page_table,
    context_len,
):
    slot_count = lax.axis_size("tensor")
    section_count = lax.axis_size("section")
    section_id = lax.axis_index("section")
    tensor_id = lax.axis_index("tensor")
    row_total, width_dev = hidden.shape
    row_dev = row_total // slot_count
    pool_pages = kv_pool.shape[1]
    gain_row = norm_gain[0].astype(jnp.float32)
    query_proj = query_weight[0]
    bias_row = query_bias[0].astype(jnp.float32)
    kv_proj = kv_weight[0]
    out_proj = out_weight[0]
    pool_layer = kv_pool[0]
    local_pages = page_table - tensor_id * pool_pages
    pieces = 1
    per_piece = row_dev // pieces
    tick_count = section_count + pieces - 1
    is_first = section_id == 0
    finished = [None] * pieces
    carried = jnp.zeros((slot_count * per_piece, width_dev), jnp.bfloat16)
    for tick_index in range(tick_count):
        if tick_index < pieces:
            blocks = hidden.reshape(slot_count, row_dev, hidden.shape[1])
            carried = jnp.where(
                is_first, blocks.reshape(slot_count * per_piece, hidden.shape[1]), carried
            )
        whole = lax.all_gather(carried, "tensor", axis=1, tiled=True)
        wide_rows = whole.astype(jnp.float32)
        mean_sq = jnp.mean(wide_rows * wide_rows, axis=1, keepdims=True)
        normed = (wide_rows * lax.rsqrt(mean_sq + epsilon) * gain_row).astype(jnp.bfloat16)
        queries = (
            jnp.dot(normed, query_proj, preferred_element_type=jnp.float32) + bias_row
        ).astype(jnp.bfloat16)
        fresh_kv = jnp.dot(normed, kv_proj, preferred_element_type=jnp.float32).astype(jnp.bfloat16)
        query_rows = lax.all_to_all(queries, "tensor", split_axis=0, concat_axis=1, tiled=True)
        fresh_rows = lax.all_to_all(fresh_kv, "tensor", split_axis=0, concat_axis=1, tiled=True)
        cached = pool_layer[local_pages].reshape(per_piece, -1, pool_layer.shape[-1])
        rotated = rotate(
            query_rows.reshape(per_piece, -1, HD).astype(jnp.float32), context_len
        ).astype(jnp.bfloat16)
        key_new = rotate(
            fresh_rows[:, : KVH * HD].reshape(per_piece, KVH, HD).astype(jnp.float32), context_len
        ).astype(jnp.bfloat16)
        value_new = fresh_rows[:, KVH * HD :].reshape(per_piece, KVH, HD)
        mixture = attend(rotated, key_new, value_new, cached, context_len)
        carried = (
            carried.astype(jnp.float32)
            + jnp.dot(
                lax.all_gather(mixture, "tensor", axis=0, tiled=True),
                out_proj,
                preferred_element_type=jnp.float32,
            )
        ).astype(jnp.bfloat16)
        if tick_index >= section_count - 1:
            finished[tick_index - section_count + 1] = carried
        if tick_index < tick_count - 1:
            carried = shifted(carried, "section", 1)
    stacked = jnp.concatenate(
        [done_part.reshape(slot_count, per_piece, width_dev) for done_part in finished], axis=1
    )
    result = stacked.reshape(row_total, width_dev)
    is_last = section_id == section_count - 1
    outgoing = jnp.where(is_last, result, jnp.zeros_like(result))[None]
    spread = lax.all_to_all(outgoing, "section", split_axis=1, concat_axis=0, tiled=True)
    return spread[section_count - 1]


def solution(mesh):
    return jax.shard_map(
        shards,
        mesh=mesh,
        in_specs=(
            P("groups", "tensor"),
            P("section", None),
            P("section", None, "tensor"),
            P("section", "tensor"),
            P("section", None, "tensor"),
            P("section", None, "tensor"),
            P("section", ("groups", "tensor"), None, None),
            P(("groups", "tensor"), None),
            P(("groups", "tensor")),
        ),
        out_specs=P(("groups", "section"), "tensor"),
        check_vma=False,
    )
```

profile of v0, /device:TPU:0, one launch (start us, length us, event | category | flops | bytes accessed | tf_op | source)
XLA Modules:
  0.0 216.4 jit_solution(4219618170490121716)
XLA Ops:
  0.0 0.9 broadcast_select_fusion
  0.9 15.1 %all_gather.24 = bf16[8,8192]{1,0:T(8,128)(2,1)S(1)} all-gather(bf16[8,2048]{1,0:T(8,128)(2,1)S(1)} %broadcast_select_fusion), channel_id=1, replica_groups=mesh['groups'=2,'tensor'=4,'section'=4] {'tensor'}, dimensions={1}, use_global_device_ids=true | all-gather | bytes 163840 | tf_op jit(solution)/shard_map/all_gather | solution.py:107
  16.0 0.8 mul.246
  17.0 0.7 bitcast_convert_fusion
  17.6 2.6 %fusion.57 = bf16[8,128]{1,0:T(8,128)(2,1)} fusion(bf16[1,8192,128]{2,1,0:T(8,128)(2,1)} %param.11, bf16[8,8192]{1,0:T(8,128)(2,1)S(1)} %all_gather.24, f32[8192]{0:T(1024)S(1)} %bitcast.174, f32[8]{0:T(128)S(1)} %add_rsqrt_fusion.3, f32[128]{0:T(128)S(1)} %bitcast_convert_fusion), kind=kOutput, calls=%fused_computation.37 | convolution fusion | flops 17041408 | bytes 2263584 | tf_op jit(solution)/shard_map/dot_general | solution.py:112
  20.3 4.7 %all-to-all-start = ((bf16[4,2,128]{2,1,0:T(2,128)(2,1)}), bf16[4,2,128]{2,1,0:T(2,128)(2,1)S(1)}, u32[]{:S(2)}, u32[]{:S(2)}) async-start(bf16[4,2,128]{2,1,0:T(2,128)(2,1)} %bitcast.3), calls=%async_computation | async-start | bytes 4096 | tf_op jit(solution)/shard_map/all_to_all | solution.py:115
  25.7 2.9 %fusion.24 = bf16[8,256]{1,0:T(8,128)(2,1)S(1)} fusion(bf16[1,8192,256]{2,1,0:T(8,128)(2,1)} %param.13, bf16[8,8192]{1,0:T(8,128)(2,1)S(1)} %all_gather.24, f32[8192]{0:T(1024)S(1)} %bitcast.175, f32[8]{0:T(128)S(1)} %add_rsqrt_fusion.3), kind=kOutput, calls=%fused_computation.26 | convolution fusion | flops 33818624 | bytes 4362272 | tf_op jit(solution)/shard_map/dot_general | solution.py:114
  28.8 0.6 all_to_all.107
  29.4 1.0 all-to-all-done
  30.4 4.1 %all-to-all-start.1 = ((bf16[4,2,256]{2,1,0:T(2,128)(2,1)}), bf16[4,2,256]{2,1,0:T(2,128)(2,1)S(1)}, u32[]{:S(2)}, u32[]{:S(2)}) async-start(bf16[4,2,256]{2,1,0:T(2,128)(2,1)} %all_to_all.107), calls=%async_computation.1 | async-start | bytes 8192 | tf_op jit(solution)/shard_map/all_to_all | solution.py:116
  34.5 5.6 %all-to-all-done.1 = bf16[4,2,256]{2,1,0:T(2,128)(2,1)S(1)} async-done(((bf16[4,2,256]{2,1,0:T(2,128)(2,1)}), bf16[4,2,256]{2,1,0:T(2,128)(2,1)S(1)}, u32[]{:S(2)}, u32[]{:S(2)}) %all-to-all-start.1) | async-done | bytes 4128 | tf_op jit(solution)/shard_map/all_to_all | solution.py:116
  41.3 11.9 %all-gather = bf16[4,2,512]{2,1,0:T(2,128)(2,1)S(1)} all-gather(bf16[1,2,512]{2,1,0:T(2,128)(2,1)S(1)} %reshape.429), channel_id=1, replica_groups=mesh['groups'=2,'tensor'=4,'section'=4] {'tensor'}, dimensions={0}, use_global_device_ids=true | all-gather | bytes 10240 | tf_op jit(solution)/shard_map/all_gather | solution.py:129
  53.6 1.4 collective-permute-start
  55.1 0.8 collective-permute-done
  55.9 13.6 %all_gather.26 = bf16[8,8192]{1,0:T(8,128)(2,1)S(1)} all-gather(bf16[8,2048]{1,0:T(8,128)(2,1)S(1)} %collective-permute-done), channel_id=1, replica_groups=mesh['groups'=2,'tensor'=4,'section'=4] {'tensor'}, dimensions={1}, use_global_device_ids=true | all-gather | bytes 163840 | tf_op jit(solution)/shard_map/all_gather | solution.py:107
  69.7 1.0 fusion.54
  70.7 3.2 %all-to-all-start.2 = ((bf16[4,2,128]{2,1,0:T(2,128)(2,1)}), bf16[4,2,128]{2,1,0:T(2,128)(2,1)S(1)}, u32[]{:S(2)}, u32[]{:S(2)}) async-start(bf16[4,2,128]{2,1,0:T(2,128)(2,1)} %bitcast.20), calls=%async_computation.2 | async-start | bytes 4096 | tf_op jit(solution)/shard_map/all_to_all | solution.py:115
  74.0 2.9 %fusion.27 = bf16[8,256]{1,0:T(8,128)(2,1)S(1)} fusion(bf16[1,8192,256]{2,1,0:T(8,128)(2,1)} %param.13, bf16[8,8192]{1,0:T(8,128)(2,1)S(1)} %all_gather.26, f32[8]{0:T(128)S(1)} %add_rsqrt_fusion.2, f32[8192]{0:T(1024)S(1)} %bitcast.177), kind=kOutput, calls=%fused_computation.27 | convolution fusion | flops 33818624 | bytes 4362272 | tf_op jit(solution)/shard_map/dot_general | solution.py:114
  76.9 0.6 all_to_all.113
  77.5 1.9 all-to-all-done.2
  79.4 3.2 %all-to-all-start.3 = ((bf16[4,2,256]{2,1,0:T(2,128)(2,1)}), bf16[4,2,256]{2,1,0:T(2,128)(2,1)S(1)}, u32[]{:S(2)}, u32[]{:S(2)}) async-start(bf16[4,2,256]{2,1,0:T(2,128)(2,1)} %all_to_all.113), calls=%async_computation.3 | async-start | bytes 8192 | tf_op jit(solution)/shard_map/all_to_all | solution.py:116
  82.6 5.5 %all-to-all-done.3 = bf16[4,2,256]{2,1,0:T(2,128)(2,1)S(1)} async-done(((bf16[4,2,256]{2,1,0:T(2,128)(2,1)}), bf16[4,2,256]{2,1,0:T(2,128)(2,1)S(1)}, u32[]{:S(2)}, u32[]{:S(2)}) %all-to-all-start.3) | async-done | bytes 4128 | tf_op jit(solution)/shard_map/all_to_all | solution.py:116
  89.4 11.9 %all-gather.1 = bf16[4,2,512]{2,1,0:T(2,128)(2,1)S(1)} all-gather(bf16[1,2,512]{2,1,0:T(2,128)(2,1)S(1)} %reshape.431), channel_id=1, replica_groups=mesh['groups'=2,'tensor'=4,'section'=4] {'tensor'}, dimensions={0}, use_global_device_ids=true | all-gather | bytes 10240 | tf_op jit(solution)/shard_map/all_gather | solution.py:129
  101.8 1.4 collective-permute-start.1
  103.2 0.8 collective-permute-done.1
  104.0 13.4 %all_gather.28 = bf16[8,8192]{1,0:T(8,128)(2,1)S(1)} all-gather(bf16[8,2048]{1,0:T(8,128)(2,1)S(1)} %collective-permute-done.1), channel_id=1, replica_groups=mesh['groups'=2,'tensor'=4,'section'=4] {'tensor'}, dimensions={1}, use_global_device_ids=true | all-gather | bytes 163840 | tf_op jit(solution)/shard_map/all_gather | solution.py:107
  117.6 1.0 fusion.51
  118.7 3.2 %all-to-all-start.4 = ((bf16[4,2,128]{2,1,0:T(2,128)(2,1)}), bf16[4,2,128]{2,1,0:T(2,128)(2,1)S(1)}, u32[]{:S(2)}, u32[]{:S(2)}) async-start(bf16[4,2,128]{2,1,0:T(2,128)(2,1)} %bitcast.33), calls=%async_computation.4 | async-start | bytes 4096 | tf_op jit(solution)/shard_map/all_to_all | solution.py:115
  121.9 2.9 %fusion.30 = bf16[8,256]{1,0:T(8,128)(2,1)S(1)} fusion(bf16[1,8192,256]{2,1,0:T(8,128)(2,1)} %param.13, bf16[8,8192]{1,0:T(8,128)(2,1)S(1)} %all_gather.28, f32[8]{0:T(128)S(1)} %add_rsqrt_fusion.1, f32[8192]{0:T(1024)S(1)} %bitcast.179), kind=kOutput, calls=%fused_computation.28 | convolution fusion | flops 33818624 | bytes 4362272 | tf_op jit(solution)/shard_map/dot_general | solution.py:114
  124.8 0.6 all_to_all.119
  125.4 1.9 all-to-all-done.4
  127.3 3.2 %all-to-all-start.5 = ((bf16[4,2,256]{2,1,0:T(2,128)(2,1)}), bf16[4,2,256]{2,1,0:T(2,128)(2,1)S(1)}, u32[]{:S(2)}, u32[]{:S(2)}) async-start(bf16[4,2,256]{2,1,0:T(2,128)(2,1)} %all_to_all.119), calls=%async_computation.5 | async-start | bytes 8192 | tf_op jit(solution)/shard_map/all_to_all | solution.py:116
  130.6 5.5 %all-to-all-done.5 = bf16[4,2,256]{2,1,0:T(2,128)(2,1)S(1)} async-done(((bf16[4,2,256]{2,1,0:T(2,128)(2,1)}), bf16[4,2,256]{2,1,0:T(2,128)(2,1)S(1)}, u32[]{:S(2)}, u32[]{:S(2)}) %all-to-all-start.5) | async-done | bytes 4128 | tf_op jit(solution)/shard_map/all_to_all | solution.py:116
  137.3 11.9 %all-gather.2 = bf16[4,2,512]{2,1,0:T(2,128)(2,1)S(1)} all-gather(bf16[1,2,512]{2,1,0:T(2,128)(2,1)S(1)} %reshape.433), channel_id=1, replica_groups=mesh['groups'=2,'tensor'=4,'section'=4] {'tensor'}, dimensions={0}, use_global_device_ids=true | all-gather | bytes 10240 | tf_op jit(solution)/shard_map/all_gather | solution.py:129
  149.7 1.3 collective-permute-start.2
  151.0 0.8 collective-permute-done.2
  151.8 13.6 %all_gather.30 = bf16[8,8192]{1,0:T(8,128)(2,1)S(1)} all-gather(bf16[8,2048]{1,0:T(8,128)(2,1)S(1)} %collective-permute-done.2), channel_id=1, replica_groups=mesh['groups'=2,'tensor'=4,'section'=4] {'tensor'}, dimensions={1}, use_global_device_ids=true | all-gather | bytes 163840 | tf_op jit(solution)/shard_map/all_gather | solution.py:107
  165.6 2.6 %fusion.48 = bf16[8,128]{1,0:T(8,128)(2,1)} fusion(bf16[1,8192,128]{2,1,0:T(8,128)(2,1)} %param.11, bf16[8,8192]{1,0:T(8,128)(2,1)S(1)} %all_gather.30, f32[8]{0:T(128)S(1)} %add_rsqrt_fusion, f32[8192]{0:T(1024)S(1)} %bitcast.180, f32[128]{0:T(128)S(1)} %bitcast_convert_fusion), kind=kOutput, calls=%fused_computation.34 | convolution fusion | flops 17041408 | bytes 2263584 | tf_op jit(solution)/shard_map/dot_general | solution.py:112
  168.2 3.2 %all-to-all-start.6 = ((bf16[4,2,128]{2,1,0:T(2,128)(2,1)}), bf16[4,2,128]{2,1,0:T(2,128)(2,1)S(1)}, u32[]{:S(2)}, u32[]{:S(2)}) async-start(bf16[4,2,128]{2,1,0:T(2,128)(2,1)} %bitcast.46), calls=%async_computation.6 | async-start | bytes 4096 | tf_op jit(solution)/shard_map/all_to_all | solution.py:115
  171.5 2.9 %fusion.33 = bf16[8,256]{1,0:T(8,128)(2,1)S(1)} fusion(bf16[1,8192,256]{2,1,0:T(8,128)(2,1)} %param.13, bf16[8,8192]{1,0:T(8,128)(2,1)S(1)} %all_gather.30, f32[8]{0:T(128)S(1)} %add_rsqrt_fusion, f32[8192]{0:T(1024)S(1)} %bitcast.181), kind=kOutput, calls=%fused_computation.29 | convolution fusion | flops 33818624 | bytes 4362272 | tf_op jit(solution)/shard_map/dot_general | solution.py:114
  174.3 0.6 all_to_all.125
  175.0 1.9 all-to-all-done.6
  176.9 3.2 %all-to-all-start.7 = ((bf16[4,2,256]{2,1,0:T(2,128)(2,1)}), bf16[4,2,256]{2,1,0:T(2,128)(2,1)S(1)}, u32[]{:S(2)}, u32[]{:S(2)}) async-start(bf16[4,2,256]{2,1,0:T(2,128)(2,1)} %all_to_all.125), calls=%async_computation.7 | async-start | bytes 8192 | tf_op jit(solution)/shard_map/all_to_all | solution.py:116
  180.1 5.5 %all-to-all-done.7 = bf16[4,2,256]{2,1,0:T(2,128)(2,1)S(1)} async-done(((bf16[4,2,256]{2,1,0:T(2,128)(2,1)}), bf16[4,2,256]{2,1,0:T(2,128)(2,1)S(1)}, u32[]{:S(2)}, u32[]{:S(2)}) %all-to-all-start.7) | async-done | bytes 4128 | tf_op jit(solution)/shard_map/all_to_all | solution.py:116
  186.9 11.9 %all-gather.3 = bf16[4,2,512]{2,1,0:T(2,128)(2,1)S(1)} all-gather(bf16[1,2,512]{2,1,0:T(2,128)(2,1)S(1)} %reshape.435), channel_id=1, replica_groups=mesh['groups'=2,'tensor'=4,'section'=4] {'tensor'}, dimensions={0}, use_global_device_ids=true | all-gather | bytes 10240 | tf_op jit(solution)/shard_map/all_gather | solution.py:129
  199.8 0.8 reduce.26
  200.7 14.9 %all_to_all.140 = bf16[4,2,2048]{2,1,0:T(2,128)(2,1)S(1)} all-to-all(bf16[4,2,2048]{2,1,0:T(2,128)(2,1)S(1)} %reshape.466), channel_id=1, replica_groups=mesh['groups'=2,'tensor'=4,'section'=4] {'section'}, dimensions={0} | all-to-all | bytes 65536 | tf_op jit(solution)/shard_map/all_to_all | solution.py:144
  215.8 0.6 slice_bitcast_fusion.2
  (107 shorter events, 8.9 us)
Async XLA Ops:
  0.0 53.2 %copy-start = (bf16[1,512,2048]{2,1,0:T(8,128)(2,1)S(1)}, bf16[1,512,2048]{2,1,0:T(8,128)(2,1)}, u32[]{:S(2)}) copy-start(bf16[1,512,2048]{2,1,0:T(8,128)(2,1)} %param.14) | copy-start | bytes 6291460
  0.0 25.0 %copy-start.4 = (s32[2,4]{1,0:T(2,128)S(1)}, s32[2,4]{1,0:T(2,128)}, u32[]{:S(2)}) copy-start(s32[2,4]{1,0:T(2,128)} %param.16) | copy-start | bytes 100
  0.0 25.1 %copy-start.3 = (bf16[1,6,16,1024]{3,2,1,0:T(8,128)(2,1)S(1)}, bf16[1,6,16,1024]{3,2,1,0:T(8,128)(2,1)}, u32[]{:S(2)}) copy-start(bf16[1,6,16,1024]{3,2,1,0:T(8,128)(2,1)} %param.15) | copy-start | bytes 589828
  20.3 10.1 %all-to-all-start = ((bf16[4,2,128]{2,1,0:T(2,128)(2,1)}), bf16[4,2,128]{2,1,0:T(2,128)(2,1)S(1)}, u32[]{:S(2)}, u32[]{:S(2)}) async-start(bf16[4,2,128]{2,1,0:T(2,128)(2,1)} %bitcast.3), calls=%async_computation | async-start | bytes 4096 | tf_op jit(solution)/shard_map/all_to_all | solution.py:115
  25.7 2.9 %copy-start.5 = (s32[2]{0:T(128)S(1)}, s32[2]{0:T(128)}, u32[]{:S(2)}) copy-start(s32[2]{0:T(128)} %param.17) | copy-start | bytes 28
  30.4 9.7 %all-to-all-start.1 = ((bf16[4,2,256]{2,1,0:T(2,128)(2,1)}), bf16[4,2,256]{2,1,0:T(2,128)(2,1)S(1)}, u32[]{:S(2)}, u32[]{:S(2)}) async-start(bf16[4,2,256]{2,1,0:T(2,128)(2,1)} %all_to_all.107), calls=%async_computation.1 | async-start | bytes 8192 | tf_op jit(solution)/shard_map/all_to_all | solution.py:116
  53.2 16.5 %copy-start.1 = (bf16[1,8192,128]{2,1,0:T(8,128)(2,1)S(1)}, bf16[1,8192,128]{2,1,0:T(8,128)(2,1)}, u32[]{:S(2)}) copy-start(bf16[1,8192,128]{2,1,0:T(8,128)(2,1)} %param.11) | copy-start | bytes 6291460
  53.6 2.3 %collective-permute-start = (bf16[8,2048]{1,0:T(8,128)(2,1)S(1)}, bf16[8,2048]{1,0:T(8,128)(2,1)S(1)}, u32[]{:S(2)}, u32[]{:S(2)}) collective-permute-start(bf16[8,2048]{1,0:T(8,128)(2,1)S(1)} %fusion.8), channel_id=1, source_target_pairs={{0,1},{1,2},{2,3},{4,5},{5,6},{6,7},{8,9},{9,10},{10,11},{12,13},{... | collective-permute-start | bytes 98312 | tf_op jit(solution)/shard_map/ppermute | solution.py:17
  70.7 8.6 %all-to-all-start.2 = ((bf16[4,2,128]{2,1,0:T(2,128)(2,1)}), bf16[4,2,128]{2,1,0:T(2,128)(2,1)S(1)}, u32[]{:S(2)}, u32[]{:S(2)}) async-start(bf16[4,2,128]{2,1,0:T(2,128)(2,1)} %bitcast.20), calls=%async_computation.2 | async-start | bytes 4096 | tf_op jit(solution)/shard_map/all_to_all | solution.py:115
  79.4 8.8 %all-to-all-start.3 = ((bf16[4,2,256]{2,1,0:T(2,128)(2,1)}), bf16[4,2,256]{2,1,0:T(2,128)(2,1)S(1)}, u32[]{:S(2)}, u32[]{:S(2)}) async-start(bf16[4,2,256]{2,1,0:T(2,128)(2,1)} %all_to_all.113), calls=%async_computation.3 | async-start | bytes 8192 | tf_op jit(solution)/shard_map/all_to_all | solution.py:116
  101.4 16.3 %copy-start.2 = (bf16[1,8192,128]{2,1,0:T(8,128)(2,1)S(1)}, bf16[1,8192,128]{2,1,0:T(8,128)(2,1)}, u32[]{:S(2)}) copy-start(bf16[1,8192,128]{2,1,0:T(8,128)(2,1)} %param.11) | copy-start | bytes 6291460
  101.8 2.3 %collective-permute-start.1 = (bf16[8,2048]{1,0:T(8,128)(2,1)S(1)}, bf16[8,2048]{1,0:T(8,128)(2,1)S(1)}, u32[]{:S(2)}, u32[]{:S(2)}) collective-permute-start(bf16[8,2048]{1,0:T(8,128)(2,1)S(1)} %add_convert_fusion.2), channel_id=1, source_target_pairs={{0,1},{1,2},{2,3},{4,5},{5,6},{6,7},{8,9},{9,10},{10,11},{12,13},{... | collective-permute-start | bytes 98312 | tf_op jit(solution)/shard_map/ppermute | solution.py:17
  118.7 8.6 %all-to-all-start.4 = ((bf16[4,2,128]{2,1,0:T(2,128)(2,1)}), bf16[4,2,128]{2,1,0:T(2,128)(2,1)S(1)}, u32[]{:S(2)}, u32[]{:S(2)}) async-start(bf16[4,2,128]{2,1,0:T(2,128)(2,1)} %bitcast.33), calls=%async_computation.4 | async-start | bytes 4096 | tf_op jit(solution)/shard_map/all_to_all | solution.py:115
  127.3 8.8 %all-to-all-start.5 = ((bf16[4,2,256]{2,1,0:T(2,128)(2,1)}), bf16[4,2,256]{2,1,0:T(2,128)(2,1)S(1)}, u32[]{:S(2)}, u32[]{:S(2)}) async-start(bf16[4,2,256]{2,1,0:T(2,128)(2,1)} %all_to_all.119), calls=%async_computation.5 | async-start | bytes 8192 | tf_op jit(solution)/shard_map/all_to_all | solution.py:116
  149.7 2.1 collective-permute-start.2
  168.2 8.6 %all-to-all-start.6 = ((bf16[4,2,128]{2,1,0:T(2,128)(2,1)}), bf16[4,2,128]{2,1,0:T(2,128)(2,1)S(1)}, u32[]{:S(2)}, u32[]{:S(2)}) async-start(bf16[4,2,128]{2,1,0:T(2,128)(2,1)} %bitcast.46), calls=%async_computation.6 | async-start | bytes 4096 | tf_op jit(solution)/shard_map/all_to_all | solution.py:115
  176.9 8.8 %all-to-all-start.7 = ((bf16[4,2,256]{2,1,0:T(2,128)(2,1)}), bf16[4,2,256]{2,1,0:T(2,128)(2,1)S(1)}, u32[]{:S(2)}, u32[]{:S(2)}) async-start(bf16[4,2,256]{2,1,0:T(2,128)(2,1)} %all_to_all.125), calls=%async_computation.7 | async-start | bytes 8192 | tf_op jit(solution)/shard_map/all_to_all | solution.py:116
where the time goes:
time: 217 us; the launch traced here: 216 us
  blocking collectives  118 us (54%)
  starting transfers between devices  32.4 us (15%)
  waiting for transfers between devices  31.4 us (14%)
  matrix products  21.6 us (10%)
  other arithmetic  7.26 us (3%)
  local copies, waits for them, and re-layouts  5.14 us (2%)
    all_gather x4, blocking collectives, shards(): whole = lax.all_gather(carried, 'tensor', axis=1, tiled=True)  55.7 us
    all_gather x4, blocking collectives, shards(): lax.all_gather(mixture, 'tensor', axis=0, tiled=True)  47.7 us
    all_to_all x4, waiting for transfers between devices, shards(): lax.all_to_all(fresh_kv, 'tensor', split_axis=0, concat_axis=1, tiled=True)  22.2 us
    all_to_all x1, blocking collectives, shards(): lax.all_to_all(outgoing, 'section', split_axis=1, concat_axis=0, tiled=True)  14.9 us
    all_to_all x4, starting transfers between devices, shards(): lax.all_to_all(queries, 'tensor', split_axis=0, concat_axis=1, tiled=True)  14.4 us
    all_to_all x4, starting transfers between devices, shards(): lax.all_to_all(fresh_kv, 'tensor', split_axis=0, concat_axis=1, tiled=True)  13.8 us
    dot_general x4, matrix products, shards(): jnp.dot(normed, kv_proj, preferred_element_type=jnp.float32)  11.5 us
    dot_general x4, matrix products, shards(): jnp.dot(normed, query_proj, preferred_element_type=jnp.float32) + bias_row  7.34 us
  transfers between devices with their start and end apart: 11, of which 11 were waited for; matrix products, arithmetic and copies ran while one was open for 6% of the time, Pallas kernels for 0%

commit v1 on v0

v1 whole, which is shorter than its diff:
```python
import functools

import jax
import jax.numpy as jnp
from jax import lax
from jax.experimental import pallas as pl
from jax.experimental.pallas import tpu as pltpu
from jax.sharding import PartitionSpec as P

HD = 128
epsilon = 1e-06
rope_base = 1000000.0
DIRECT_PEERS = 8
VMEM = pl.BlockSpec(memory_space=pltpu.VMEM)
SMEM = pl.BlockSpec(memory_space=pltpu.SMEM)


def round_up(value, unit):
    return -(-value // unit) * unit


def kernel_call(body, outs, in_specs, scratch=(), many=True):
    specs = [VMEM] * len(outs)
    return pl.pallas_call(
        body,
        out_shape=outs if many else outs[0],
        in_specs=in_specs,
        out_specs=specs if many else specs[0],
        scratch_shapes=list(scratch),
    )


class Ring:
    def __init__(self):
        self.count = lax.axis_size("tensor")
        self.sections = lax.axis_size("section")
        self.direct = self.count <= DIRECT_PEERS
        me = lax.axis_index("tensor")
        order = jnp.arange(self.count, dtype=jnp.int32)
        self.sources = (me - order) % self.count if self.direct else order
        self.targets = (me + order) % self.count if self.direct else order

    def send(self, value, pairs, step):
        n = self.count
        m = self.sections
        perm = [(t * m + a, (t + step) % n * m + b) for a, b in pairs for t in range(n)]
        return lax.ppermute(value, ("tensor", "section"), perm)

    def gather(self, value, origin, target):
        if self.direct:
            got = [] if origin != target else [value]
            first = len(got)
            return got + [
                self.send(value, [(origin, target)], step) for step in range(first, self.count)
            ]
        if origin != target:
            value = lax.ppermute(value, "section", [(origin, target)])
        whole = lax.all_gather(value, "tensor", axis=0, tiled=False)
        return [whole[slot] for slot in range(self.count)]

    def trade(self, values):
        if self.direct:
            every = [(s, s) for s in range(self.sections)]
            return [values[0]] + [
                self.send(values[step], every, step) for step in range(1, self.count)
            ]
        swapped = lax.all_to_all(
            jnp.stack(values), "tensor", split_axis=0, concat_axis=0, tiled=True
        )
        return [swapped[slot] for slot in range(self.count)]


def pack_kernel(info, tensor_ref, targets, table, context, pool, *outs):
    n, heads_dev, group, kv_heads, width, page_len = info
    tokens = pool.shape[0]
    pages = tokens // page_len
    row_dev, blocks = table.shape
    extra = outs[0].shape[0] - tokens
    lane = lax.broadcasted_iota(jnp.int32, (extra, 2 * width), 1)
    row = lax.broadcasted_iota(jnp.int32, (extra, 2 * width), 0)
    first = tensor_ref[0] * pages
    aux = jnp.zeros((extra, 2 * width), jnp.float32)
    for j in range(row_dev):
        length = context[j]
        uses = jnp.zeros((extra, 2 * width), jnp.float32)
        for b in range(blocks):
            offset = lane - (table[j, b] - first) * page_len
            inside = (offset >= 0) & (offset < page_len) & (offset + b * page_len < length)
            uses = uses + jnp.where(inside, 1.0, 0.0)
        aux = jnp.where(row == j, uses, aux)
        aux = jnp.where(row == row_dev + j, length.astype(jnp.float32), aux)
    aux = aux.astype(jnp.bfloat16)
    for k in range(n):
        head = (targets[k] * heads_dev) // group * HD
        key_at = pl.multiple_of(head, HD)
        value_at = pl.multiple_of(head + kv_heads * HD, HD)
        outs[k][0:tokens, 0:width] = pool[:, pl.ds(key_at, width)]
        outs[k][0:tokens, width : 2 * width] = pool[:, pl.ds(value_at, width)]
        outs[k][tokens:, :] = aux


def unpack_kernel(info, sources, frequency, *refs):
    n, row_dev, tokens = info
    packs = refs[:n]
    counts, cosine, sine, lengths = refs[n:]
    counts[...] = jnp.zeros_like(counts)
    for k in range(n):
        aux = packs[k][tokens:, :].astype(jnp.float32)
        base = sources[k] * row_dev
        for j in range(row_dev):
            counts[k, pl.ds(base + j, 1), :] = aux[j : j + 1, :tokens]
            lengths[pl.ds(base + j, 1), :] = aux[row_dev + j : row_dev + j + 1, :HD]
    angles = lengths[...] * frequency[...]
    lane = lax.broadcasted_iota(jnp.int32, angles.shape, 1)
    cosine[...] = jnp.cos(angles)
    sine[...] = jnp.where(lane < HD // 2, -1.0, 1.0) * jnp.sin(angles)


def rotate(values, cosine, sine):
    swapped = jnp.concatenate([values[:, HD // 2 :], values[:, : HD // 2]], axis=1)
    return values * cosine + swapped * sine


def project_kernel(info, sources, gain, wq, wkv, bias, counts, cosine, sine, *refs):
    n, heads_dev, group, tokens, width = info
    pieces = refs[:n]
    packs = refs[n : 2 * n]
    out = refs[2 * n]
    slice_len = pieces[0].shape[1]
    features = n * slice_len
    wide = [piece[...].astype(jnp.float32) for piece in pieces]
    total = functools.reduce(
        jnp.add, [jnp.sum(value * value, axis=1, keepdims=True) for value in wide]
    )
    inverse = lax.rsqrt(total * (1.0 / features) + epsilon)
    queries = None
    for k in range(n):
        at = pl.multiple_of(sources[k] * slice_len, HD)
        scale = gain[:, pl.ds(at, slice_len)].astype(jnp.float32)
        normed = (wide[k] * inverse * scale).astype(jnp.bfloat16)
        q_part = jnp.dot(normed, wq[pl.ds(at, slice_len), :], preferred_element_type=jnp.float32)
        kv_part = jnp.dot(normed, wkv[pl.ds(at, slice_len), :], preferred_element_type=jnp.float32)
        queries = q_part if queries is None else queries + q_part
        fresh = kv_part if k == 0 else fresh + kv_part
    queries = (queries + bias[...].astype(jnp.float32)).astype(jnp.bfloat16).astype(jnp.float32)
    span = heads_dev * HD
    out[:, 3 * span : 3 * span + fresh.shape[1]] = fresh.astype(jnp.bfloat16).astype(jnp.float32)
    for i in range(heads_dev):
        head = slice(i * HD, (i + 1) * HD)
        rotated = rotate(queries[:, head], cosine[...], sine[...]).astype(jnp.bfloat16)
        key_at = (i // group) * HD
        scores = []
        for k in range(n):
            keys = packs[k][0:tokens, key_at : key_at + HD]
            scores.append(
                lax.dot_general(
                    rotated, keys, (((1,), (1,)), ((), ())), preferred_element_type=jnp.float32
                )
                * HD ** (-0.5)
            )
        tops = [
            jnp.where(counts[k] > 0.0, scores[k], -1e30) for k in range(n)
        ]
        top = functools.reduce(
            jnp.maximum, [jnp.max(value, axis=1, keepdims=True) for value in tops]
        )
        mass = 0.0
        mixed = 0.0
        for k in range(n):
            weight = counts[k] * jnp.exp(tops[k] - top)
            mass = mass + jnp.sum(weight, axis=1, keepdims=True)
            values = packs[k][0:tokens, width + key_at : width + key_at + HD]
            mixed = mixed + jnp.dot(
                weight.astype(jnp.bfloat16), values, preferred_element_type=jnp.float32
            )
        out[:, i * HD : (i + 1) * HD] = rotated.astype(jnp.float32)
        out[:, span + i * HD : span + (i + 1) * HD] = mixed / mass
        out[:, 2 * span + i * HD : 2 * span + (i + 1) * HD] = jnp.broadcast_to(
            top + jnp.log(mass), (mixed.shape[0], HD)
        )


def output_kernel(info, sources, own, wout, cosine, sine, *refs):
    n, heads_dev, group, kv_heads, kv_width, splits = info
    parts = refs[:n]
    outs = refs[n : n + splits]
    slots, fresh = refs[n + splits :]
    span = heads_dev * HD
    for k in range(n):
        slots[sources[k]] = parts[k][...]
    for j in range(n):
        fresh[:, j * kv_width : (j + 1) * kv_width] = slots[j, :, 3 * span : 3 * span + kv_width]
    keys = []
    for h in range(kv_heads):
        key = rotate(fresh[:, h * HD : (h + 1) * HD], cosine[...], sine[...])
        keys.append(key.astype(jnp.bfloat16).astype(jnp.float32))
    mixture = []
    for h in range(n * heads_dev):
        j, i = divmod(h, heads_dev)
        kv = h // group
        query = slots[j, :, i * HD : (i + 1) * HD]
        cached = slots[j, :, span + i * HD : span + (i + 1) * HD]
        level = slots[j, :, 2 * span + i * HD : 2 * span + (i + 1) * HD]
        value = fresh[:, (kv_heads + kv) * HD : (kv_heads + kv + 1) * HD]
        score = jnp.sum(query * keys[kv], axis=1, keepdims=True) * HD ** (-0.5)
        weight = 1.0 / (1.0 + jnp.exp(level - score))
        mixture.append((cached + weight * (value - cached)).astype(jnp.bfloat16))
    mixture = jnp.concatenate(mixture, axis=1)
    stream = own[...].astype(jnp.float32) + jnp.dot(
        mixture, wout[...], preferred_element_type=jnp.float32
    )
    stream = stream.astype(jnp.bfloat16)
    rows = stream.shape[0] // splits
    for part in range(splits):
        outs[part][...] = stream[part * rows : (part + 1) * rows]


def shards(
    hidden,
    norm_gain,
    query_weight,
    query_bias,
    kv_weight,
    out_weight,
    kv_pool,
    page_table,
    context_len,
):
    ring = Ring()
    n = ring.count
    sections = ring.sections
    section_id = lax.axis_index("section")
    tensor_id = lax.axis_index("tensor")
    rows, slice_len = hidden.shape
    row_dev = page_table.shape[0]
    page_len = kv_pool.shape[2]
    tokens = kv_pool.shape[1] * page_len
    wq, wkv, wout = query_weight[0], kv_weight[0], out_weight[0]
    heads_dev = wq.shape[1] // HD
    kv_width = wkv.shape[1]
    kv_heads = kv_pool.shape[3] // (2 * HD)
    group = heads_dev * n // kv_heads
    width = max(1, heads_dev // group) * HD
    f32, bf16 = jnp.float32, jnp.bfloat16

    pieces = ring.gather(hidden, 0, 0)

    extra = round_up(2 * row_dev, 16)
    pack_info = (n, heads_dev, group, kv_heads, width, page_len)
    packs = kernel_call(
        functools.partial(pack_kernel, pack_info),
        [jax.ShapeDtypeStruct((tokens + extra, 2 * width), bf16)] * n,
        [SMEM] * 4 + [VMEM],
    )(
        tensor_id.reshape(1),
        ring.targets,
        page_table,
        context_len,
        kv_pool.reshape(tokens, kv_pool.shape[3]),
    )
    packs = ring.trade(packs)
    frequency = rope_base ** (-(jnp.arange(HD // 2, dtype=f32) * 2.0) / HD)
    frequency = jnp.concatenate([frequency, frequency])[None, :]
    counts, cosine, sine = kernel_call(
        functools.partial(unpack_kernel, (n, row_dev, tokens)),
        [
            jax.ShapeDtypeStruct((n, rows, tokens), f32),
            jax.ShapeDtypeStruct((rows, HD), f32),
            jax.ShapeDtypeStruct((rows, HD), f32),
        ],
        [SMEM, VMEM] + [VMEM] * n,
        [pltpu.VMEM((rows, HD), f32)],
    )(ring.sources, frequency, *packs)

    message = 3 * heads_dev * HD + round_up(kv_width, HD)
    project = kernel_call(
        functools.partial(project_kernel, (n, heads_dev, group, tokens, width)),
        [jax.ShapeDtypeStruct((rows, message), f32)],
        [SMEM] + [VMEM] * (7 + 2 * n),
        many=False,
    )
    for layer in range(sections):
        sent = project(
            ring.sources, norm_gain, wq, wkv, query_bias, counts, cosine, sine, *pieces, *packs
        )
        parts = ring.gather(sent, layer, layer)
        splits = sections if layer == sections - 1 else 1
        own = pieces[0] if ring.direct else pieces_own(pieces, tensor_id)
        stream = kernel_call(
            functools.partial(
                output_kernel, (n, heads_dev, group, kv_heads, kv_width, splits)
            ),
            [jax.ShapeDtypeStruct((rows // splits, slice_len), bf16)] * splits,
            [SMEM] + [VMEM] * (4 + n),
            [pltpu.VMEM((n, rows, message), f32), pltpu.VMEM((rows, n * kv_width), f32)],
        )(ring.sources, own, wout, cosine, sine, *parts)
        if layer < sections - 1:
            pieces = ring.gather(stream[0], layer, layer + 1)
    last = sections - 1
    result = jnp.where(section_id == last, stream[last], jnp.zeros_like(stream[last]))
    for target in range(last):
        result = result + lax.ppermute(stream[target], "section", [(last, target)])
    return result


def pieces_own(pieces, tensor_id):
    return lax.dynamic_index_in_dim(jnp.stack(pieces), tensor_id, 0, keepdims=False)


def solution(mesh):
    return jax.shard_map(
        shards,
        mesh=mesh,
        in_specs=(
            P("groups", "tensor"),
            P("section", None),
            P("section", None, "tensor"),
            P("section", "tensor"),
            P("section", None, "tensor"),
            P("section", None, "tensor"),
            P("section", ("groups", "tensor"), None, None),
            P(("groups", "tensor"), None),
            P(("groups", "tensor")),
        ),
        out_specs=P(("groups", "section"), "tensor"),
        check_vma=False,
    )
```

time: 217 us -> 143 us (0.66)
  blocking collectives: 118 us -> 0 us
  Pallas kernels: 0 us -> 34.3 us
  matrix products: 21.6 us -> 0 us
  waiting for transfers between devices: 31.4 us -> 51.8 us
  starting transfers between devices: 32.4 us -> 44.3 us
  other arithmetic: 7.26 us -> 2.39 us
  local copies, waits for them, and re-layouts: 5.14 us -> 8.51 us
    all_gather x8 -> x0, blocking collectives: 103 us -> none  [the longest x4 55.7 us: shards(): whole = lax.all_gather(carried, 'tensor', axis=1, tiled=True)]
    ppermute x3 -> x33, waiting for transfers between devices: 2.52 us -> 51.8 us  [the longest x3 40.5 us: shards(): result = result + lax.ppermute(stream[target], 'section', [(last, target)])]
    ppermute x3 -> x33, starting transfers between devices: 4.12 us -> 44.3 us  [the longest x30 41.7 us: send(): return lax.ppermute(value, ('tensor', 'section'), perm)]
    pallas_call x0 -> x10, Pallas kernels: none -> 34.3 us  [the longest x4 20 us: shards(): project(ring.sources, norm_gain, wq, wkv, query_bias, counts, cosine, sin...]
    all_to_all x8 -> x0, waiting for transfers between devices: 28.9 us -> none  [the longest x4 22.2 us: shards(): lax.all_to_all(fresh_kv, 'tensor', split_axis=0, concat_axis=1, tiled=True)]
    all_to_all x8 -> x0, starting transfers between devices: 28.2 us -> none  [the longest x4 14.4 us: shards(): lax.all_to_all(queries, 'tensor', split_axis=0, concat_axis=1, tiled=True)]
    dot_general x20 -> x0, matrix products: 21.6 us -> none  [the longest x4 11.5 us: shards(): jnp.dot(normed, kv_proj, preferred_element_type=jnp.float32)]
    all_to_all x1 -> x0, blocking collectives: 14.9 us -> none  [shards(): lax.all_to_all(outgoing, 'section', split_axis=1, concat_axis=0, tiled=True)]
  transfers between devices with their start and end apart: 11 -> 33, of which waited for: 11 -> 7; matrix products, arithmetic and copies ran while one was open for 6% -> 1% of each run, Pallas kernels for 0% -> 2%
where the time goes in v1:
time: 143 us; the launch traced here: 142 us
  waiting for transfers between devices  51.8 us (36%)
  starting transfers between devices  44.3 us (31%)
  Pallas kernels  34.3 us (24%)
  local copies, waits for them, and re-layouts  8.51 us (6%)
  other arithmetic  2.39 us (2%)
    ppermute x30, starting transfers between devices, send(): return lax.ppermute(value, ('tensor', 'section'), perm)  41.7 us
    ppermute x3, waiting for transfers between devices, shards(): result = result + lax.ppermute(stream[target], 'section', [(last, target)])  40.5 us
    pallas_call x4, Pallas kernels, shards(): project(ring.sources, norm_gain, wq, wkv, query_bias, counts, cosine, sin...  20 us
    ppermute x30, waiting for transfers between devices, send(): return lax.ppermute(value, ('tensor', 'section'), perm)  11.2 us
    pallas_call x4, Pallas kernels, shards(): kernel_call(functools.partial(output_kernel, (n, heads_dev, group, kv_hea...  11 us
    unnamed x60, local copies, waits for them, and re-layouts  8.51 us
  transfers between devices with their start and end apart: 33, of which 7 were waited for; matrix products, arithmetic and copies ran while one was open for 1% of the time, Pallas kernels for 2%

profile of v1, /device:TPU:0, one launch (start us, length us, event | category | flops | bytes accessed | tf_op | source)
XLA Modules:
  0.0 141.9 jit_solution(6370487644540976749)
XLA Ops:
  0.0 7.0 %collective-permute-start.5 = (bf16[8,2048]{1,0:T(8,128)(2,1)}, bf16[8,2048]{1,0:T(8,128)(2,1)S(1)}, u32[]{:S(2)}, u32[]{:S(2)}) collective-permute-start(bf16[8,2048]{1,0:T(8,128)(2,1)} %own.1), channel_id=1, source_target_pairs={{0,12},{4,0},{8,4},{12,8},{16,28},{20,16},{24,20},{28,24}} | collective-permute-start | bytes 98312 | tf_op jit(solution)/shard_map/ppermute | solution.py:47
  7.0 1.9 %collective-permute-start.4 = (bf16[8,2048]{1,0:T(8,128)(2,1)}, bf16[8,2048]{1,0:T(8,128)(2,1)S(1)}, u32[]{:S(2)}, u32[]{:S(2)}) collective-permute-start(bf16[8,2048]{1,0:T(8,128)(2,1)} %own.1), channel_id=1, source_target_pairs={{0,8},{4,12},{8,0},{12,4},{16,24},{20,28},{24,16},{28,20}} | collective-permute-start | bytes 98312 | tf_op jit(solution)/shard_map/ppermute | solution.py:47
  8.9 2.9 %collective-permute-start.3 = (bf16[8,2048]{1,0:T(8,128)(2,1)}, bf16[8,2048]{1,0:T(8,128)(2,1)S(1)}, u32[]{:S(2)}, u32[]{:S(2)}) collective-permute-start(bf16[8,2048]{1,0:T(8,128)(2,1)} %own.1), channel_id=1, source_target_pairs={{0,4},{4,8},{8,12},{12,0},{16,20},{20,24},{24,28},{28,16}} | collective-permute-start | bytes 98312 | tf_op jit(solution)/shard_map/ppermute | solution.py:47
  12.4 1.7 %shard_map.91 = (bf16[112,256]{1,0:T(8,128)(2,1)}, bf16[112,256]{1,0:T(8,128)(2,1)}, bf16[112,256]{1,0:T(8,128)(2,1)}, bf16[112,256]{1,0:T(8,128)(2,1)}) custom-call(s32[1]{0:T(128)} %bitcast.2.tensor_ref, s32[4]{0:T(128)} %and_select_fusion.targets, s32[2,4]{1,0:T(2,128)} %table.1, s32[2]{0:T(128)} %context.1, bf16[96,1024]{1,0:T(8,128)(2,1)} %bitcast.19), custom_call_target="tpu_custom_call" | custom-call | tf_op jit(solution)/shard_map/pallas_call | solution.py:250
  14.2 2.5 %collective-permute-start = (bf16[112,256]{1,0:T(8,128)(2,1)}, bf16[112,256]{1,0:T(8,128)(2,1)S(1)}, u32[]{:S(2)}, u32[]{:S(2)}) collective-permute-start(bf16[112,256]{1,0:T(8,128)(2,1)} %get-tuple-element.17), channel_id=1, source_target_pairs={{0,4},{4,8},{8,12},{12,0},{1,5},{5,9},{9,13},{13,1},{2,6},{6,10},{... | collective-permute-start | bytes 172040 | tf_op jit(solution)/shard_map/ppermute | solution.py:47
  16.6 0.9 collective-permute-start.1
  18.1 2.2 %collective-permute-done.refs_1_.refs_5_ = bf16[112,256]{1,0:T(8,128)(2,1)S(1)} collective-permute-done((bf16[112,256]{1,0:T(8,128)(2,1)}, bf16[112,256]{1,0:T(8,128)(2,1)S(1)}, u32[]{:S(2)}, u32[]{:S(2)}) %collective-permute-start) | collective-permute-done | bytes 57376 | tf_op jit(solution)/shard_map/ppermute | solution.py:47
  20.3 1.0 collective-permute-start.2
  22.0 2.7 %collective-permute-done.2.refs_3_.refs_7_ = bf16[112,256]{1,0:T(8,128)(2,1)S(1)} collective-permute-done((bf16[112,256]{1,0:T(8,128)(2,1)}, bf16[112,256]{1,0:T(8,128)(2,1)S(1)}, u32[]{:S(2)}, u32[]{:S(2)}) %collective-permute-start.2) | collective-permute-done | bytes 57376 | tf_op jit(solution)/shard_map/ppermute | solution.py:47
  25.4 1.6 %shard_map.92 = (f32[4,8,96]{2,1,0:T(8,128)}, f32[8,128]{1,0:T(8,128)}, f32[8,128]{1,0:T(8,128)}) custom-call(s32[4]{0:T(128)} %and_select_fusion.1.sources, f32[1,128]{1,0:T(1,128)} %maximum_bitcast_fusion.frequency, bf16[112,256]{1,0:T(8,128)(2,1)} %get-tuple-element.16.refs_0_.refs_4_, bf16[112,256]{1,0:T(8,128)(2,1)} %copy-done, ...), custom_call_target="tpu_custom_call" | custom-call | tf_op jit(solution)/shard_map/pallas_call | solution.py:264
  27.6 5.0 %shard_map.93.refs_0_ = f32[8,640]{1,0:T(8,128)} custom-call(s32[4]{0:T(128)} %and_select_fusion.1.sources, bf16[1,8192]{1,0:T(2,128)(2,1)} %gain.7, bf16[8192,128]{1,0:T(8,128)(2,1)} %bitcast.15, bf16[8192,256]{1,0:T(8,128)(2,1)} %bitcast.7, bf16[1,128]{1,0:T(2,128)(2,1)} %bias.7, f32[4,8,96]{2,1,0:T(8,128)} %get-tuple-element.22.counts, ...), custom_call_target="tpu_custom_call" | custom-call | tf_op jit(solution)/shard_map/pallas_call | solution.py:283
  32.6 4.7 %collective-permute-start.8 = (f32[8,640]{1,0:T(8,128)}, f32[8,640]{1,0:T(8,128)S(1)}, u32[]{:S(2)}, u32[]{:S(2)}) collective-permute-start(f32[8,640]{1,0:T(8,128)} %shard_map.93.refs_0_), channel_id=1, source_target_pairs={{0,12},{4,0},{8,4},{12,8},{16,28},{20,16},{24,20},{28,24}} | collective-permute-start | bytes 61448 | tf_op jit(solution)/shard_map/ppermute | solution.py:47
  37.3 1.9 %collective-permute-start.7 = (f32[8,640]{1,0:T(8,128)}, f32[8,640]{1,0:T(8,128)S(1)}, u32[]{:S(2)}, u32[]{:S(2)}) collective-permute-start(f32[8,640]{1,0:T(8,128)} %shard_map.93.refs_0_), channel_id=1, source_target_pairs={{0,8},{4,12},{8,0},{12,4},{16,24},{20,28},{24,16},{28,20}} | collective-permute-start | bytes 61448 | tf_op jit(solution)/shard_map/ppermute | solution.py:47
  39.2 2.5 %collective-permute-start.6 = (f32[8,640]{1,0:T(8,128)}, f32[8,640]{1,0:T(8,128)S(1)}, u32[]{:S(2)}, u32[]{:S(2)}) collective-permute-start(f32[8,640]{1,0:T(8,128)} %shard_map.93.refs_0_), channel_id=1, source_target_pairs={{0,4},{4,8},{8,12},{12,0},{16,20},{20,24},{24,28},{28,16}} | collective-permute-start | bytes 61448 | tf_op jit(solution)/shard_map/ppermute | solution.py:47
  41.7 2.4 %collective-permute-done.7.refs_2_ = f32[8,640]{1,0:T(8,128)S(1)} collective-permute-done((f32[8,640]{1,0:T(8,128)}, f32[8,640]{1,0:T(8,128)S(1)}, u32[]{:S(2)}, u32[]{:S(2)}) %collective-permute-start.7) | collective-permute-done | bytes 20512 | tf_op jit(solution)/shard_map/ppermute | solution.py:47
  44.1 2.8 %collective-permute-done.6.refs_1_ = f32[8,640]{1,0:T(8,128)S(1)} collective-permute-done((f32[8,640]{1,0:T(8,128)}, f32[8,640]{1,0:T(8,128)S(1)}, u32[]{:S(2)}, u32[]{:S(2)}) %collective-permute-start.6) | collective-permute-done | bytes 20512 | tf_op jit(solution)/shard_map/ppermute | solution.py:47
  47.5 2.8 %shard_map.94 = bf16[8,2048]{1,0:T(8,128)(2,1)} custom-call(s32[4]{0:T(128)} %and_select_fusion.1.sources, bf16[8,2048]{1,0:T(8,128)(2,1)} %own.1, bf16[512,2048]{1,0:T(8,128)(2,1)} %bitcast.11, f32[8,128]{1,0:T(8,128)} %get-tuple-element.20.cosine, f32[8,128]{1,0:T(8,128)} %get-tuple-element.21.sine, f32[8,640]{1,0:T(8,128)} %shard_map.93.refs_0_, ...), custom_call_target="tpu_custom_call" | custom-call | tf_op jit(solution)/shard_map/pallas_call | solution.py:289
  50.3 1.3 collective-permute-start.12
  51.6 1.3 collective-permute-start.11
  52.9 1.3 collective-permute-start.10
  54.2 1.3 collective-permute-start.9
  57.3 5.0 %shard_map.95.refs_0_ = f32[8,640]{1,0:T(8,128)} custom-call(s32[4]{0:T(128)} %and_select_fusion.1.sources, bf16[1,8192]{1,0:T(2,128)(2,1)} %gain.7, bf16[8192,128]{1,0:T(8,128)(2,1)} %bitcast.16, bf16[8192,256]{1,0:T(8,128)(2,1)} %bitcast.8, bf16[1,128]{1,0:T(2,128)(2,1)} %bias.7, f32[4,8,96]{2,1,0:T(8,128)} %get-tuple-element.22.counts, ...), custom_call_target="tpu_custom_call" | custom-call | tf_op jit(solution)/shard_map/pallas_call | solution.py:283
  62.3 0.7 collective-permute-start.15
  62.9 0.7 collective-permute-start.14
  63.6 0.7 collective-permute-start.13
  65.5 2.7 %shard_map.96 = bf16[8,2048]{1,0:T(8,128)(2,1)} custom-call(s32[4]{0:T(128)} %and_select_fusion.1.sources, bf16[8,2048]{1,0:T(8,128)(2,1)} %copy-done.4, bf16[512,2048]{1,0:T(8,128)(2,1)} %bitcast.12, f32[8,128]{1,0:T(8,128)} %get-tuple-element.20.cosine, f32[8,128]{1,0:T(8,128)} %get-tuple-element.21.sine, f32[8,640]{1,0:T(8,128)} %shard_map.95.refs_0_, ...), custom_call_target="tpu_custom_call" | custom-call | tf_op jit(solution)/shard_map/pallas_call | solution.py:289
  68.2 0.7 collective-permute-start.19
  68.9 0.7 collective-permute-start.18
  69.6 0.7 collective-permute-start.17
  70.2 0.7 collective-permute-start.16
  72.2 5.0 %shard_map.97.refs_0_ = f32[8,640]{1,0:T(8,128)} custom-call(s32[4]{0:T(128)} %and_select_fusion.1.sources, bf16[1,8192]{1,0:T(2,128)(2,1)} %gain.7, bf16[8192,128]{1,0:T(8,128)(2,1)} %bitcast.17, bf16[8192,256]{1,0:T(8,128)(2,1)} %bitcast.9, bf16[1,128]{1,0:T(2,128)(2,1)} %bias.7, f32[4,8,96]{2,1,0:T(8,128)} %get-tuple-element.22.counts, ...), custom_call_target="tpu_custom_call" | custom-call | tf_op jit(solution)/shard_map/pallas_call | solution.py:283
  77.2 0.7 collective-permute-start.22
  77.8 0.7 collective-permute-start.21
  78.5 0.7 collective-permute-start.20
  80.4 2.8 %shard_map.98 = bf16[8,2048]{1,0:T(8,128)(2,1)} custom-call(s32[4]{0:T(128)} %and_select_fusion.1.sources, bf16[8,2048]{1,0:T(8,128)(2,1)} %copy-done.5, bf16[512,2048]{1,0:T(8,128)(2,1)} %bitcast.13, f32[8,128]{1,0:T(8,128)} %get-tuple-element.20.cosine, f32[8,128]{1,0:T(8,128)} %get-tuple-element.21.sine, f32[8,640]{1,0:T(8,128)} %shard_map.97.refs_0_, ...), custom_call_target="tpu_custom_call" | custom-call | tf_op jit(solution)/shard_map/pallas_call | solution.py:289
  83.2 0.7 collective-permute-start.26
  83.8 0.7 collective-permute-start.25
  84.5 0.7 collective-permute-start.24
  85.2 0.7 collective-permute-start.23
  87.1 5.0 %shard_map.99.refs_0_ = f32[8,640]{1,0:T(8,128)} custom-call(s32[4]{0:T(128)} %and_select_fusion.1.sources, bf16[1,8192]{1,0:T(2,128)(2,1)} %gain.7, bf16[8192,128]{1,0:T(8,128)(2,1)} %bitcast.18, bf16[8192,256]{1,0:T(8,128)(2,1)} %bitcast.10, bf16[1,128]{1,0:T(2,128)(2,1)} %bias.7, f32[4,8,96]{2,1,0:T(8,128)} %get-tuple-element.22.counts, ...), custom_call_target="tpu_custom_call" | custom-call | tf_op jit(solution)/shard_map/pallas_call | solution.py:283
  92.1 0.7 collective-permute-start.29
  92.8 0.7 collective-permute-start.28
  93.4 0.7 collective-permute-start.27
  95.3 2.8 %shard_map.100 = (bf16[2,2048]{1,0:T(2,128)(2,1)}, bf16[2,2048]{1,0:T(2,128)(2,1)}, bf16[2,2048]{1,0:T(2,128)(2,1)}, bf16[2,2048]{1,0:T(2,128)(2,1)}) custom-call(s32[4]{0:T(128)} %and_select_fusion.1.sources, bf16[8,2048]{1,0:T(8,128)(2,1)} %copy-done.3, bf16[512,2048]{1,0:T(8,128)(2,1)} %bitcast.14, f32[8,128]{1,0:T(8,128)} %get-tuple-element.20.cosine, ...), custom_call_target="tpu_custom_call" | custom-call | tf_op jit(solution)/shard_map/pallas_call | solution.py:289
  98.1 1.3 collective-permute-start.30
  99.4 0.7 collective-permute-start.31
  100.1 0.7 collective-permute-start.32
  100.7 40.5 %collective-permute-done.30 = bf16[2,2048]{1,0:T(2,128)(2,1)S(1)} collective-permute-done((bf16[2,2048]{1,0:T(2,128)(2,1)}, bf16[2,2048]{1,0:T(2,128)(2,1)S(1)}, u32[]{:S(2)}, u32[]{:S(2)}) %collective-permute-start.30) | collective-permute-done | bytes 8224 | tf_op jit(solution)/shard_map/ppermute | solution.py:302
  (93 shorter events, 12.0 us)
Async XLA Ops:
  0.0 26.9 %collective-permute-start.5 = (bf16[8,2048]{1,0:T(8,128)(2,1)}, bf16[8,2048]{1,0:T(8,128)(2,1)S(1)}, u32[]{:S(2)}, u32[]{:S(2)}) collective-permute-start(bf16[8,2048]{1,0:T(8,128)(2,1)} %own.1), channel_id=1, source_target_pairs={{0,12},{4,0},{8,4},{12,8},{16,28},{20,16},{24,20},{28,24}} | collective-permute-start | bytes 98312 | tf_op jit(solution)/shard_map/ppermute | solution.py:47
  7.0 20.0 %collective-permute-start.4 = (bf16[8,2048]{1,0:T(8,128)(2,1)}, bf16[8,2048]{1,0:T(8,128)(2,1)S(1)}, u32[]{:S(2)}, u32[]{:S(2)}) collective-permute-start(bf16[8,2048]{1,0:T(8,128)(2,1)} %own.1), channel_id=1, source_target_pairs={{0,8},{4,12},{8,0},{12,4},{16,24},{20,28},{24,16},{28,20}} | collective-permute-start | bytes 98312 | tf_op jit(solution)/shard_map/ppermute | solution.py:47
  8.9 18.0 %collective-permute-start.3 = (bf16[8,2048]{1,0:T(8,128)(2,1)}, bf16[8,2048]{1,0:T(8,128)(2,1)S(1)}, u32[]{:S(2)}, u32[]{:S(2)}) collective-permute-start(bf16[8,2048]{1,0:T(8,128)(2,1)} %own.1), channel_id=1, source_target_pairs={{0,4},{4,8},{8,12},{12,0},{16,20},{20,24},{24,28},{28,16}} | collective-permute-start | bytes 98312 | tf_op jit(solution)/shard_map/ppermute | solution.py:47
  14.2 6.2 %collective-permute-start = (bf16[112,256]{1,0:T(8,128)(2,1)}, bf16[112,256]{1,0:T(8,128)(2,1)S(1)}, u32[]{:S(2)}, u32[]{:S(2)}) collective-permute-start(bf16[112,256]{1,0:T(8,128)(2,1)} %get-tuple-element.17), channel_id=1, source_target_pairs={{0,4},{4,8},{8,12},{12,0},{1,5},{5,9},{9,13},{13,1},{2,6},{6,10},{... | collective-permute-start | bytes 172040 | tf_op jit(solution)/shard_map/ppermute | solution.py:47
  16.6 5.3 %collective-permute-start.1 = (bf16[112,256]{1,0:T(8,128)(2,1)}, bf16[112,256]{1,0:T(8,128)(2,1)S(1)}, u32[]{:S(2)}, u32[]{:S(2)}) collective-permute-start(bf16[112,256]{1,0:T(8,128)(2,1)} %get-tuple-element.18), channel_id=1, source_target_pairs={{0,8},{4,12},{8,0},{12,4},{1,9},{5,13},{9,1},{13,5},{2,10},{6,14},... | collective-permute-start | bytes 172040 | tf_op jit(solution)/shard_map/ppermute | solution.py:47
  20.3 4.4 %copy-start = (bf16[112,256]{1,0:T(8,128)(2,1)}, bf16[112,256]{1,0:T(8,128)(2,1)S(1)}, u32[]{:S(2)}) copy-start(bf16[112,256]{1,0:T(8,128)(2,1)S(1)} %collective-permute-done.refs_1_.refs_5_) | copy-start | bytes 172036
  20.3 4.4 %collective-permute-start.2 = (bf16[112,256]{1,0:T(8,128)(2,1)}, bf16[112,256]{1,0:T(8,128)(2,1)S(1)}, u32[]{:S(2)}, u32[]{:S(2)}) collective-permute-start(bf16[112,256]{1,0:T(8,128)(2,1)} %get-tuple-element.19), channel_id=1, source_target_pairs={{0,12},{4,0},{8,4},{12,8},{1,13},{5,1},{9,5},{13,9},{2,14},{6,2},{... | collective-permute-start | bytes 172040 | tf_op jit(solution)/shard_map/ppermute | solution.py:47
  22.0 2.8 %copy-start.1 = (bf16[112,256]{1,0:T(8,128)(2,1)}, bf16[112,256]{1,0:T(8,128)(2,1)S(1)}, u32[]{:S(2)}) copy-start(bf16[112,256]{1,0:T(8,128)(2,1)S(1)} %collective-permute-done.1.refs_2_.refs_6_) | copy-start | bytes 172036
  24.7 0.6 copy-start.2
  26.9 0.6 copy-start.6
  26.9 0.6 copy-start.7
  27.0 0.6 copy-start.8
  32.6 9.1 %collective-permute-start.8 = (f32[8,640]{1,0:T(8,128)}, f32[8,640]{1,0:T(8,128)S(1)}, u32[]{:S(2)}, u32[]{:S(2)}) collective-permute-start(f32[8,640]{1,0:T(8,128)} %shard_map.93.refs_0_), channel_id=1, source_target_pairs={{0,12},{4,0},{8,4},{12,8},{16,28},{20,16},{24,20},{28,24}} | collective-permute-start | bytes 61448 | tf_op jit(solution)/shard_map/ppermute | solution.py:47
  37.3 6.8 %collective-permute-start.7 = (f32[8,640]{1,0:T(8,128)}, f32[8,640]{1,0:T(8,128)S(1)}, u32[]{:S(2)}, u32[]{:S(2)}) collective-permute-start(f32[8,640]{1,0:T(8,128)} %shard_map.93.refs_0_), channel_id=1, source_target_pairs={{0,8},{4,12},{8,0},{12,4},{16,24},{20,28},{24,16},{28,20}} | collective-permute-start | bytes 61448 | tf_op jit(solution)/shard_map/ppermute | solution.py:47
  39.2 7.7 %collective-permute-start.6 = (f32[8,640]{1,0:T(8,128)}, f32[8,640]{1,0:T(8,128)S(1)}, u32[]{:S(2)}, u32[]{:S(2)}) collective-permute-start(f32[8,640]{1,0:T(8,128)} %shard_map.93.refs_0_), channel_id=1, source_target_pairs={{0,4},{4,8},{8,12},{12,0},{16,20},{20,24},{24,28},{28,16}} | collective-permute-start | bytes 61448 | tf_op jit(solution)/shard_map/ppermute | solution.py:47
  41.7 5.2 %copy-start.23 = (f32[8,640]{1,0:T(8,128)}, f32[8,640]{1,0:T(8,128)S(1)}, u32[]{:S(2)}) copy-start(f32[8,640]{1,0:T(8,128)S(1)} %collective-permute-done.8.refs_3_) | copy-start | bytes 61444
  44.1 2.8 %copy-start.26 = (f32[8,640]{1,0:T(8,128)}, f32[8,640]{1,0:T(8,128)S(1)}, u32[]{:S(2)}) copy-start(f32[8,640]{1,0:T(8,128)S(1)} %collective-permute-done.7.refs_2_) | copy-start | bytes 61444
  50.3 5.2 %collective-permute-start.12 = (bf16[8,2048]{1,0:T(8,128)(2,1)}, bf16[8,2048]{1,0:T(8,128)(2,1)S(1)}, u32[]{:S(2)}, u32[]{:S(2)}) collective-permute-start(bf16[8,2048]{1,0:T(8,128)(2,1)} %shard_map.94), channel_id=1, source_target_pairs={{0,13},{4,1},{8,5},{12,9},{16,29},{20,17},{24,21},{28,25}} | collective-permute-start | bytes 98312 | tf_op jit(solution)/shard_map/ppermute | solution.py:47
  51.6 3.9 %collective-permute-start.11 = (bf16[8,2048]{1,0:T(8,128)(2,1)}, bf16[8,2048]{1,0:T(8,128)(2,1)S(1)}, u32[]{:S(2)}, u32[]{:S(2)}) collective-permute-start(bf16[8,2048]{1,0:T(8,128)(2,1)} %shard_map.94), channel_id=1, source_target_pairs={{0,9},{4,13},{8,1},{12,5},{16,25},{20,29},{24,17},{28,21}} | collective-permute-start | bytes 98312 | tf_op jit(solution)/shard_map/ppermute | solution.py:47
  52.9 3.2 %collective-permute-start.10 = (bf16[8,2048]{1,0:T(8,128)(2,1)}, bf16[8,2048]{1,0:T(8,128)(2,1)S(1)}, u32[]{:S(2)}, u32[]{:S(2)}) collective-permute-start(bf16[8,2048]{1,0:T(8,128)(2,1)} %shard_map.94), channel_id=1, source_target_pairs={{0,5},{4,9},{8,13},{12,1},{16,21},{20,25},{24,29},{28,17}} | collective-permute-start | bytes 98312 | tf_op jit(solution)/shard_map/ppermute | solution.py:47
  54.2 2.4 %collective-permute-start.9 = (bf16[8,2048]{1,0:T(8,128)(2,1)}, bf16[8,2048]{1,0:T(8,128)(2,1)S(1)}, u32[]{:S(2)}, u32[]{:S(2)}) collective-permute-start(bf16[8,2048]{1,0:T(8,128)(2,1)} %shard_map.94), channel_id=1, source_target_pairs={{0,1},{4,5},{8,9},{12,13},{16,17},{20,21},{24,25},{28,29}} | collective-permute-start | bytes 98312 | tf_op jit(solution)/shard_map/ppermute | solution.py:47
  55.5 1.0 copy-start.11
  55.5 1.0 copy-start.14
  62.3 2.0 %collective-permute-start.15 = (f32[8,640]{1,0:T(8,128)}, f32[8,640]{1,0:T(8,128)S(1)}, u32[]{:S(2)}, u32[]{:S(2)}) collective-permute-start(f32[8,640]{1,0:T(8,128)} %shard_map.95.refs_0_), channel_id=1, source_target_pairs={{1,13},{5,1},{9,5},{13,9},{17,29},{21,17},{25,21},{29,25}} | collective-permute-start | bytes 61448 | tf_op jit(solution)/shard_map/ppermute | solution.py:47
  62.9 1.4 collective-permute-start.14
  63.6 0.7 collective-permute-start.13
  68.2 2.7 %collective-permute-start.19 = (bf16[8,2048]{1,0:T(8,128)(2,1)}, bf16[8,2048]{1,0:T(8,128)(2,1)S(1)}, u32[]{:S(2)}, u32[]{:S(2)}) collective-permute-start(bf16[8,2048]{1,0:T(8,128)(2,1)} %shard_map.96), channel_id=1, source_target_pairs={{1,14},{5,2},{9,6},{13,10},{17,30},{21,18},{25,22},{29,26}} | collective-permute-start | bytes 98312 | tf_op jit(solution)/shard_map/ppermute | solution.py:47
  68.9 2.0 %collective-permute-start.18 = (bf16[8,2048]{1,0:T(8,128)(2,1)}, bf16[8,2048]{1,0:T(8,128)(2,1)S(1)}, u32[]{:S(2)}, u32[]{:S(2)}) collective-permute-start(bf16[8,2048]{1,0:T(8,128)(2,1)} %shard_map.96), channel_id=1, source_target_pairs={{1,10},{5,14},{9,2},{13,6},{17,26},{21,30},{25,18},{29,22}} | collective-permute-start | bytes 98312 | tf_op jit(solution)/shard_map/ppermute | solution.py:47
  69.6 1.4 collective-permute-start.17
  70.2 0.7 collective-permute-start.16
  70.9 0.6 copy-start.12
  71.0 0.6 copy-start.17
  71.6 0.6 copy-start.5
  77.2 2.0 %collective-permute-start.22 = (f32[8,640]{1,0:T(8,128)}, f32[8,640]{1,0:T(8,128)S(1)}, u32[]{:S(2)}, u32[]{:S(2)}) collective-permute-start(f32[8,640]{1,0:T(8,128)} %shard_map.97.refs_0_), channel_id=1, source_target_pairs={{2,14},{6,2},{10,6},{14,10},{18,30},{22,18},{26,22},{30,26}} | collective-permute-start | bytes 61448 | tf_op jit(solution)/shard_map/ppermute | solution.py:47
  77.8 1.4 collective-permute-start.21
  78.5 0.7 collective-permute-start.20
  83.2 2.7 %collective-permute-start.26 = (bf16[8,2048]{1,0:T(8,128)(2,1)}, bf16[8,2048]{1,0:T(8,128)(2,1)S(1)}, u32[]{:S(2)}, u32[]{:S(2)}) collective-permute-start(bf16[8,2048]{1,0:T(8,128)(2,1)} %shard_map.98), channel_id=1, source_target_pairs={{2,15},{6,3},{10,7},{14,11},{18,31},{22,19},{26,23},{30,27}} | collective-permute-start | bytes 98312 | tf_op jit(solution)/shard_map/ppermute | solution.py:47
  83.8 2.0 %collective-permute-start.25 = (bf16[8,2048]{1,0:T(8,128)(2,1)}, bf16[8,2048]{1,0:T(8,128)(2,1)S(1)}, u32[]{:S(2)}, u32[]{:S(2)}) collective-permute-start(bf16[8,2048]{1,0:T(8,128)(2,1)} %shard_map.98), channel_id=1, source_target_pairs={{2,11},{6,15},{10,3},{14,7},{18,27},{22,31},{26,19},{30,23}} | collective-permute-start | bytes 98312 | tf_op jit(solution)/shard_map/ppermute | solution.py:47
  84.5 1.4 collective-permute-start.24
  85.2 0.7 collective-permute-start.23
  85.9 0.6 copy-start.10
  85.9 0.6 copy-start.13
  92.1 2.0 %collective-permute-start.29 = (f32[8,640]{1,0:T(8,128)}, f32[8,640]{1,0:T(8,128)S(1)}, u32[]{:S(2)}, u32[]{:S(2)}) collective-permute-start(f32[8,640]{1,0:T(8,128)} %shard_map.99.refs_0_), channel_id=1, source_target_pairs={{3,15},{7,3},{11,7},{15,11},{19,31},{23,19},{27,23},{31,27}} | collective-permute-start | bytes 61448 | tf_op jit(solution)/shard_map/ppermute | solution.py:47
  92.8 1.4 collective-permute-start.28
  93.4 0.7 collective-permute-start.27
  98.1 43.2 %collective-permute-start.30 = (bf16[2,2048]{1,0:T(2,128)(2,1)}, bf16[2,2048]{1,0:T(2,128)(2,1)S(1)}, u32[]{:S(2)}, u32[]{:S(2)}) collective-permute-start(bf16[2,2048]{1,0:T(2,128)(2,1)} %get-tuple-element.24), channel_id=1, source_target_pairs={{3,0},{7,4},{11,8},{15,12},{19,16},{23,20},{27,24},{31,28}} | collective-permute-start | bytes 24584 | tf_op jit(solution)/shard_map/ppermute | solution.py:302
  99.4 41.9 %collective-permute-start.31 = (bf16[2,2048]{1,0:T(2,128)(2,1)}, bf16[2,2048]{1,0:T(2,128)(2,1)S(1)}, u32[]{:S(2)}, u32[]{:S(2)}) collective-permute-start(bf16[2,2048]{1,0:T(2,128)(2,1)} %get-tuple-element.25), channel_id=1, source_target_pairs={{3,1},{7,5},{11,9},{15,13},{19,17},{23,21},{27,25},{31,29}} | collective-permute-start | bytes 24584 | tf_op jit(solution)/shard_map/ppermute | solution.py:302
  100.1 41.2 %collective-permute-start.32 = (bf16[2,2048]{1,0:T(2,128)(2,1)}, bf16[2,2048]{1,0:T(2,128)(2,1)S(1)}, u32[]{:S(2)}, u32[]{:S(2)}) collective-permute-start(bf16[2,2048]{1,0:T(2,128)(2,1)} %get-tuple-element.26), channel_id=1, source_target_pairs={{3,2},{7,6},{11,10},{15,14},{19,18},{23,22},{27,26},{31,30}} | collective-permute-start | bytes 24584 | tf_op jit(solution)/shard_map/ppermute | solution.py:302
  (15 other events, 9.0 us)

commit v2 on v1

v2 whole, which is shorter than its diff:
```python
import functools

import jax
import jax.numpy as jnp
from jax import lax
from jax.experimental import pallas as pl
from jax.experimental.pallas import tpu as pltpu
from jax.sharding import PartitionSpec as P

HD = 128
epsilon = 1e-06
rope_base = 1000000.0
DIRECT_PEERS = 8
KERNEL_VMEM = 24 * 2**20
VMEM = pl.BlockSpec(memory_space=pltpu.VMEM)
SMEM = pl.BlockSpec(memory_space=pltpu.SMEM)


def round_up(value, unit):
    return -(-value // unit) * unit


def kernel_call(body, outs, in_specs, scratch=(), many=True):
    specs = [VMEM] * len(outs)
    call = pl.pallas_call(
        body,
        out_shape=outs if many else outs[0],
        in_specs=in_specs,
        out_specs=specs if many else specs[0],
        scratch_shapes=list(scratch),
        compiler_params=pltpu.CompilerParams(vmem_limit_bytes=KERNEL_VMEM),
    )

    def placed(*operands):
        return call(
            *[
                pltpu.with_memory_space_constraint(value, pltpu.VMEM) if spec is VMEM else value
                for value, spec in zip(operands, in_specs)
            ]
        )

    return placed


class Ring:
    def __init__(self):
        self.count = lax.axis_size("tensor")
        self.sections = lax.axis_size("section")
        self.direct = self.count <= DIRECT_PEERS
        me = lax.axis_index("tensor")
        order = jnp.arange(self.count, dtype=jnp.int32)
        self.sources = (me - order) % self.count if self.direct else order

    def send(self, value, origin, target, step):
        n, m = self.count, self.sections
        perm = [(t * m + origin, (t + step) % n * m + target) for t in range(n)]
        return lax.ppermute(value, ("tensor", "section"), perm)

    def advance(self, value, origin, target):
        if self.direct:
            return [self.send(value, origin, target, step) for step in range(self.count)]
        value = lax.ppermute(value, "section", [(origin, target)])
        whole = lax.all_gather(value, "tensor", axis=0, tiled=False)
        return [whole[slot] for slot in range(self.count)]

    def trade(self, values):
        return lax.all_to_all(values, "tensor", split_axis=0, concat_axis=0, tiled=True)


def pack_kernel(info, tensor_ref, table, context, pool, hidden, out):
    n, heads_dev, group, kv_heads, width, page_len, extra = info
    tokens = pool.shape[0]
    pages = tokens // page_len
    row_dev, blocks = table.shape
    lane = lax.broadcasted_iota(jnp.int32, (extra, 2 * width), 1)
    row = lax.broadcasted_iota(jnp.int32, (extra, 2 * width), 0)
    first = tensor_ref[0] * pages
    aux = jnp.zeros((extra, 2 * width), jnp.float32)
    for j in range(row_dev):
        length = context[j]
        uses = jnp.zeros((extra, 2 * width), jnp.float32)
        for b in range(blocks):
            offset = lane - (table[j, b] - first) * page_len
            inside = (offset >= 0) & (offset < page_len) & (offset + b * page_len < length)
            uses = uses + jnp.where(inside, 1.0, 0.0)
        aux = jnp.where(row == j, uses, aux)
        aux = jnp.where(row == row_dev + j, length.astype(jnp.float32), aux)
    aux = aux.astype(jnp.bfloat16)
    rows, slice_len = hidden.shape
    strips = slice_len // (2 * width)
    stream = hidden[...]
    stream = [stream[:, c * 2 * width : (c + 1) * 2 * width] for c in range(strips)]
    stream = jnp.concatenate(stream, axis=0)
    for k in range(n):
        head = k * heads_dev // group * HD
        out[k, 0:tokens, 0:width] = pool[:, head : head + width]
        head = head + kv_heads * HD
        out[k, 0:tokens, width : 2 * width] = pool[:, head : head + width]
        out[k, tokens : tokens + extra, :] = aux
        out[k, tokens + extra :, :] = stream


def unpack_kernel(info, frequency, packs, counts, cosine, sine, wide, lengths):
    n, row_dev, tokens, extra = info
    counts[...] = jnp.zeros_like(counts)
    rows, features = wide.shape
    slice_len = features // n
    strip = packs.shape[2]
    for k in range(n):
        aux = packs[k, tokens : tokens + extra, :].astype(jnp.float32)
        base = k * row_dev
        for j in range(row_dev):
            counts[k, base + j : base + j + 1, :] = aux[j : j + 1, :tokens]
            lengths[base + j : base + j + 1, :] = aux[row_dev + j : row_dev + j + 1, :HD]
        for c in range(slice_len // strip):
            at = tokens + extra + c * rows
            to = k * slice_len + c * strip
            wide[:, to : to + strip] = packs[k, at : at + rows, :]
    angles = lengths[...] * frequency[...]
    lane = lax.broadcasted_iota(jnp.int32, angles.shape, 1)
    cosine[...] = jnp.cos(angles)
    sine[...] = jnp.where(lane < HD // 2, -1.0, 1.0) * jnp.sin(angles)


def rotate(values, cosine, sine):
    swapped = jnp.concatenate([values[:, HD // 2 :], values[:, : HD // 2]], axis=1)
    return values * cosine + swapped * sine


def project_kernel(info, sources, gain, wq, wkv, bias, counts, cosine, sine, *refs):
    n, heads_dev, group, tokens, width = info
    packs, *pieces, out = refs
    features = gain.shape[1]
    slice_len = features // n
    if len(pieces) == n:
        wide = [piece[...].astype(jnp.float32) for piece in pieces]
        starts = [pl.multiple_of(sources[k] * slice_len, HD) for k in range(n)]
    else:
        starts = [k * slice_len for k in range(n)]
        wide = [pieces[0][:, at : at + slice_len].astype(jnp.float32) for at in starts]
    total = functools.reduce(
        jnp.add, [jnp.sum(value * value, axis=1, keepdims=True) for value in wide]
    )
    inverse = lax.rsqrt(total * (1.0 / features) + epsilon)
    queries = None
    for k in range(n):
        at = starts[k]
        scale = gain[:, pl.ds(at, slice_len)].astype(jnp.float32)
        normed = (wide[k] * inverse * scale).astype(jnp.bfloat16)
        q_part = jnp.dot(normed, wq[pl.ds(at, slice_len), :], preferred_element_type=jnp.float32)
        kv_part = jnp.dot(normed, wkv[pl.ds(at, slice_len), :], preferred_element_type=jnp.float32)
        queries = q_part if queries is None else queries + q_part
        fresh = kv_part if k == 0 else fresh + kv_part
    queries = (queries + bias[...].astype(jnp.float32)).astype(jnp.bfloat16).astype(jnp.float32)
    span = heads_dev * HD
    out[0, :, 3 * span : 3 * span + fresh.shape[1]] = fresh.astype(jnp.bfloat16).astype(jnp.float32)
    for i in range(heads_dev):
        head = slice(i * HD, (i + 1) * HD)
        rotated = rotate(queries[:, head], cosine[...], sine[...]).astype(jnp.bfloat16)
        key_at = (i // group) * HD
        scores = []
        for k in range(n):
            keys = packs[k, 0:tokens, key_at : key_at + HD]
            scores.append(
                lax.dot_general(
                    rotated, keys, (((1,), (1,)), ((), ())), preferred_element_type=jnp.float32
                )
                * HD ** (-0.5)
            )
        tops = [
            jnp.where(counts[k] > 0.0, scores[k], -1e30) for k in range(n)
        ]
        top = functools.reduce(
            jnp.maximum, [jnp.max(value, axis=1, keepdims=True) for value in tops]
        )
        mass = 0.0
        mixed = 0.0
        for k in range(n):
            weight = counts[k] * jnp.exp(tops[k] - top)
            mass = mass + jnp.sum(weight, axis=1, keepdims=True)
            values = packs[k, 0:tokens, width + key_at : width + key_at + HD]
            mixed = mixed + jnp.dot(
                weight.astype(jnp.bfloat16), values, preferred_element_type=jnp.float32
            )
        out[0, :, i * HD : (i + 1) * HD] = rotated.astype(jnp.float32)
        out[0, :, span + i * HD : span + (i + 1) * HD] = mixed / mass
        out[0, :, 2 * span + i * HD : 2 * span + (i + 1) * HD] = jnp.broadcast_to(
            top + jnp.log(mass), (mixed.shape[0], HD)
        )
    for k in range(1, n):
        out[k] = out[0]


def output_kernel(info, own, wout, cosine, sine, slots, *refs):
    n, heads_dev, group, kv_heads, kv_width, splits = info
    outs = refs[:splits]
    fresh = refs[splits]
    span = heads_dev * HD
    for j in range(n):
        fresh[:, j * kv_width : (j + 1) * kv_width] = slots[j, :, 3 * span : 3 * span + kv_width]
    keys = []
    for h in range(kv_heads):
        key = rotate(fresh[:, h * HD : (h + 1) * HD], cosine[...], sine[...])
        keys.append(key.astype(jnp.bfloat16).astype(jnp.float32))
    mixture = []
    for h in range(n * heads_dev):
        j, i = divmod(h, heads_dev)
        kv = h // group
        query = slots[j, :, i * HD : (i + 1) * HD]
        cached = slots[j, :, span + i * HD : span + (i + 1) * HD]
        level = slots[j, :, 2 * span + i * HD : 2 * span + (i + 1) * HD]
        value = fresh[:, (kv_heads + kv) * HD : (kv_heads + kv + 1) * HD]
        score = jnp.sum(query * keys[kv], axis=1, keepdims=True) * HD ** (-0.5)
        weight = 1.0 / (1.0 + jnp.exp(level - score))
        mixture.append((cached + weight * (value - cached)).astype(jnp.bfloat16))
    mixture = jnp.concatenate(mixture, axis=1)
    stream = own[...].astype(jnp.float32) + jnp.dot(
        mixture, wout[...], preferred_element_type=jnp.float32
    )
    stream = stream.astype(jnp.bfloat16)
    rows = stream.shape[0] // splits
    for part in range(splits):
        outs[part][...] = stream[part * rows : (part + 1) * rows]


def shards(
    hidden,
    norm_gain,
    query_weight,
    query_bias,
    kv_weight,
    out_weight,
    kv_pool,
    page_table,
    context_len,
):
    ring = Ring()
    n = ring.count
    sections = ring.sections
    section_id = lax.axis_index("section")
    tensor_id = lax.axis_index("tensor")
    rows, slice_len = hidden.shape
    row_dev = page_table.shape[0]
    page_len = kv_pool.shape[2]
    tokens = kv_pool.shape[1] * page_len
    wq, wkv, wout = query_weight[0], kv_weight[0], out_weight[0]
    heads_dev = wq.shape[1] // HD
    kv_width = wkv.shape[1]
    kv_heads = kv_pool.shape[3] // (2 * HD)
    group = heads_dev * n // kv_heads
    width = max(1, heads_dev // group) * HD
    f32, bf16 = jnp.float32, jnp.bfloat16

    extra = round_up(2 * row_dev, 16)
    pack_info = (n, heads_dev, group, kv_heads, width, page_len, extra)
    height = tokens + extra + rows * slice_len // (2 * width)
    packs = kernel_call(
        functools.partial(pack_kernel, pack_info),
        [jax.ShapeDtypeStruct((n, height, 2 * width), bf16)],
        [SMEM] * 3 + [VMEM] * 2,
        many=False,
    )(
        tensor_id.reshape(1),
        page_table,
        context_len,
        kv_pool.reshape(tokens, kv_pool.shape[3]),
        hidden,
    )
    packs = ring.trade(packs)
    frequency = rope_base ** (-(jnp.arange(HD // 2, dtype=f32) * 2.0) / HD)
    frequency = jnp.concatenate([frequency, frequency])[None, :]
    counts, cosine, sine, first = kernel_call(
        functools.partial(unpack_kernel, (n, row_dev, tokens, extra)),
        [
            jax.ShapeDtypeStruct((n, rows, tokens), f32),
            jax.ShapeDtypeStruct((rows, HD), f32),
            jax.ShapeDtypeStruct((rows, HD), f32),
            jax.ShapeDtypeStruct((rows, n * slice_len), bf16),
        ],
        [VMEM] * 2,
        [pltpu.VMEM((rows, HD), f32)],
    )(frequency, packs)

    message = 3 * heads_dev * HD + round_up(kv_width, HD)
    pieces = [first]
    own = hidden
    for layer in range(sections):
        sent = kernel_call(
            functools.partial(project_kernel, (n, heads_dev, group, tokens, width)),
            [jax.ShapeDtypeStruct((n, rows, message), f32)],
            [SMEM] + [VMEM] * (8 + len(pieces)),
            many=False,
        )(ring.sources, norm_gain, wq, wkv, query_bias, counts, cosine, sine, packs, *pieces)
        parts = ring.trade(sent)
        splits = sections if layer == sections - 1 else 1
        stream = kernel_call(
            functools.partial(
                output_kernel, (n, heads_dev, group, kv_heads, kv_width, splits)
            ),
            [jax.ShapeDtypeStruct((rows // splits, slice_len), bf16)] * splits,
            [VMEM] * 5,
            [pltpu.VMEM((rows, n * kv_width), f32)],
        )(own, wout, cosine, sine, parts)
        if layer < sections - 1:
            pieces = ring.advance(stream[0], layer, layer + 1)
            own = pieces[0] if ring.direct else pieces_own(pieces, tensor_id)
    last = sections - 1
    result = jnp.where(section_id == last, stream[last], jnp.zeros_like(stream[last]))
    for target in range(last):
        result = result + lax.ppermute(stream[target], "section", [(last, target)])
    return result


def pieces_own(pieces, tensor_id):
    return lax.dynamic_index_in_dim(jnp.stack(pieces), tensor_id, 0, keepdims=False)


def solution(mesh):
    return jax.shard_map(
        shards,
        mesh=mesh,
        in_specs=(
            P("groups", "tensor"),
            P("section", None),
            P("section", None, "tensor"),
            P("section", "tensor"),
            P("section", None, "tensor"),
            P("section", None, "tensor"),
            P("section", ("groups", "tensor"), None, None),
            P(("groups", "tensor"), None),
            P(("groups", "tensor")),
        ),
        out_specs=P(("groups", "section"), "tensor"),
        check_vma=False,
    )
```

time: 143 us -> 99.6 us (0.70)
  blocking collectives: 0 us -> 33.1 us
  waiting for transfers between devices: 51.8 us -> 25.1 us
  starting transfers between devices: 44.3 us -> 19.5 us
  Pallas kernels: 34.3 us -> 11.4 us
  other arithmetic: 2.39 us -> 0.72 us
    all_to_all x0 -> x4, blocking collectives: none -> 33.1 us  [trade(): lax.all_to_all(values, 'tensor', split_axis=0, concat_axis=0, tiled=True)]
    ppermute x30 -> x12, starting transfers between devices: 41.7 us -> 10.5 us  [send(): return lax.ppermute(value, ('tensor', 'section'), perm)]
    ppermute x3, waiting for transfers between devices: 40.5 us -> 12.6 us  [shards(): result = result + lax.ppermute(stream[target], 'section', [(last, target)])]
    pallas_call x10, Pallas kernels: 34.3 us -> 11.4 us  [placed(): call(*[pltpu.with_memory_space_constraint(value, pltpu.VMEM) if spec is V...]
    all_to_all x0 -> x1, waiting for transfers between devices: none -> 10.9 us  [trade(): lax.all_to_all(values, 'tensor', split_axis=0, concat_axis=0, tiled=True)]
    ppermute x30 -> x12, waiting for transfers between devices: 11.2 us -> 1.58 us  [send(): return lax.ppermute(value, ('tensor', 'section'), perm)]
    all_to_all x0 -> x1, starting transfers between devices: none -> 6.35 us  [trade(): lax.all_to_all(values, 'tensor', split_axis=0, concat_axis=0, tiled=True)]
    unnamed x60 -> x24, local copies, waits for them, and re-layouts: 8.51 us -> 8.22 us
  transfers between devices with their start and end apart: 33 -> 16, of which waited for: 7 -> 4; matrix products, arithmetic and copies ran while one was open for 1% -> 0% of each run, Pallas kernels for 2% -> 0%
where the time goes in v2:
time: 99.6 us; the launch traced here: 98.2 us
  blocking collectives  33.1 us (33%)
  waiting for transfers between devices  25.1 us (25%)
  starting transfers between devices  19.5 us (20%)
  Pallas kernels  11.4 us (11%)
  local copies, waits for them, and re-layouts  8.22 us (8%)
    all_to_all x4, blocking collectives, trade(): lax.all_to_all(values, 'tensor', split_axis=0, concat_axis=0, tiled=True)  33.1 us
    ppermute x3, waiting for transfers between devices, shards(): result = result + lax.ppermute(stream[target], 'section', [(last, target)])  12.6 us
    pallas_call x10, Pallas kernels, placed(): call(*[pltpu.with_memory_space_constraint(value, pltpu.VMEM) if spec is V...  11.4 us
    all_to_all x1, waiting for transfers between devices, trade(): lax.all_to_all(values, 'tensor', split_axis=0, concat_axis=0, tiled=True)  10.9 us
    ppermute x12, starting transfers between devices, send(): return lax.ppermute(value, ('tensor', 'section'), perm)  10.5 us
    unnamed x24, local copies, waits for them, and re-layouts  8.22 us
    all_to_all x1, starting transfers between devices, trade(): lax.all_to_all(values, 'tensor', split_axis=0, concat_axis=0, tiled=True)  6.35 us
    ppermute x3, starting transfers between devices, shards(): result = result + lax.ppermute(stream[target], 'section', [(last, target)])  2.63 us
  transfers between devices with their start and end apart: 16, of which 4 were waited for; matrix products, arithmetic and copies ran while one was open for 0% of the time, Pallas kernels for 0%

profile of v2, /device:TPU:0, one launch (start us, length us, event | category | flops | bytes accessed | tf_op | source)
XLA Modules:
  0.0 98.2 jit_solution(9861000553709737372)
XLA Ops:
  0.0 0.9 copy-done.6
  0.9 0.8 copy-done.7
  1.7 0.7 copy-done.10
  2.4 0.7 copy-done.11
  3.0 1.3 %shard_map.91 = bf16[4,176,256]{2,1,0:T(8,128)(2,1)} custom-call(s32[1]{0:T(128)} %bitcast.2.tensor_ref, s32[2,4]{1,0:T(2,128)S(1)} %copy-done.10, s32[2]{0:T(128)S(1)} %copy-done.11, bf16[96,1024]{1,0:T(8,128)(2,1)S(1)} %bitcast.19, bf16[8,2048]{1,0:T(8,128)(2,1)S(1)} %copy-done.7), custom_call_target="tpu_custom_call" | custom-call | tf_op jit(solution)/shard_map/pallas_call | solution.py:35
  4.4 6.3 %all-to-all-start = ((bf16[4,176,256]{2,1,0:T(8,128)(2,1)}), bf16[4,176,256]{2,1,0:T(8,128)(2,1)S(1)}, u32[]{:S(2)}, u32[]{:S(2)}) async-start(bf16[4,176,256]{2,1,0:T(8,128)(2,1)} %shard_map.91), calls=%async_computation | async-start | bytes 720896 | tf_op jit(solution)/shard_map/all_to_all | solution.py:67
  10.7 0.1 maximum_bitcast_fusion.frequency
  10.8 10.9 %all-to-all-done.packs.refs_0_ = bf16[4,176,256]{2,1,0:T(8,128)(2,1)S(1)} async-done(((bf16[4,176,256]{2,1,0:T(8,128)(2,1)}), bf16[4,176,256]{2,1,0:T(8,128)(2,1)S(1)}, u32[]{:S(2)}, u32[]{:S(2)}) %all-to-all-start) | async-done | bytes 360480 | tf_op jit(solution)/shard_map/all_to_all | solution.py:67
  21.7 0.1 shard_map.92
  21.7 0.0 copy-start
  21.8 2.2 %copy-done = bf16[1,8192,256]{2,1,0:T(8,128)(2,1)S(1)} copy-done((bf16[1,8192,256]{2,1,0:T(8,128)(2,1)S(1)}, bf16[1,8192,256]{2,1,0:T(8,128)(2,1)}, u32[]{:S(2)}) %copy-start) | copy-done | bytes 4194328
  23.9 1.6 %copy-done.2 = bf16[1,8192,128]{2,1,0:T(8,128)(2,1)S(1)} copy-done((bf16[1,8192,128]{2,1,0:T(8,128)(2,1)S(1)}, bf16[1,8192,128]{2,1,0:T(8,128)(2,1)}, u32[]{:S(2)}) %copy-start.2) | copy-done | bytes 2097176
  25.5 0.8 copy-done.5
  26.3 0.7 copy-done.9
  27.0 2.0 %shard_map.93 = f32[4,8,640]{2,1,0:T(8,128)S(1)} custom-call(s32[4]{0:T(128)S(1)} %and_select_fusion.sources, bf16[1,8192]{1,0:T(2,128)(2,1)S(1)} %copy-done.5, bf16[8192,128]{1,0:T(8,128)(2,1)S(1)} %bitcast.11, bf16[8192,256]{1,0:T(8,128)(2,1)S(1)} %bitcast.7, bf16[1,128]{1,0:T(2,128)(2,1)S(1)} %copy-done.9, f32[4,8,96]{2,1,0:T(8,128)S(1)} %get-tuple-element.15.counts, ...), custom_call_target="tpu_custom_call" | custom-call | tf_op jit(solution)/shard_map/pallas_call | solution.py:35
  28.9 8.5 %all_to_all.25.slots = f32[4,8,640]{2,1,0:T(8,128)S(1)} all-to-all(f32[4,8,640]{2,1,0:T(8,128)S(1)} %shard_map.93), channel_id=1, replica_groups=mesh['groups'=2,'tensor'=4,'section'=4] {'tensor'}, dimensions={0} | all-to-all | bytes 163840 | tf_op jit(solution)/shard_map/all_to_all | solution.py:67
  37.4 0.5 shard_map.94
  37.9 1.3 %collective-permute-start = (bf16[8,2048]{1,0:T(8,128)(2,1)S(1)}, bf16[8,2048]{1,0:T(8,128)(2,1)S(1)}, u32[]{:S(2)}, u32[]{:S(2)}) collective-permute-start(bf16[8,2048]{1,0:T(8,128)(2,1)S(1)} %shard_map.94), channel_id=1, source_target_pairs={{0,1},{4,5},{8,9},{12,13},{16,17},{20,21},{24,25},{28,29}} | collective-permute-start | bytes 98312 | tf_op jit(solution)/shard_map/ppermute | solution.py:57
  39.2 1.3 %collective-permute-start.1 = (bf16[8,2048]{1,0:T(8,128)(2,1)S(1)}, bf16[8,2048]{1,0:T(8,128)(2,1)S(1)}, u32[]{:S(2)}, u32[]{:S(2)}) collective-permute-start(bf16[8,2048]{1,0:T(8,128)(2,1)S(1)} %shard_map.94), channel_id=1, source_target_pairs={{0,5},{4,9},{8,13},{12,1},{16,21},{20,25},{24,29},{28,17}} | collective-permute-start | bytes 98312 | tf_op jit(solution)/shard_map/ppermute | solution.py:57
  40.5 1.3 %collective-permute-start.2 = (bf16[8,2048]{1,0:T(8,128)(2,1)S(1)}, bf16[8,2048]{1,0:T(8,128)(2,1)S(1)}, u32[]{:S(2)}, u32[]{:S(2)}) collective-permute-start(bf16[8,2048]{1,0:T(8,128)(2,1)S(1)} %shard_map.94), channel_id=1, source_target_pairs={{0,9},{4,13},{8,1},{12,5},{16,25},{20,29},{24,17},{28,21}} | collective-permute-start | bytes 98312 | tf_op jit(solution)/shard_map/ppermute | solution.py:57
  41.8 1.3 %collective-permute-start.3 = (bf16[8,2048]{1,0:T(8,128)(2,1)S(1)}, bf16[8,2048]{1,0:T(8,128)(2,1)S(1)}, u32[]{:S(2)}, u32[]{:S(2)}) collective-permute-start(bf16[8,2048]{1,0:T(8,128)(2,1)S(1)} %shard_map.94), channel_id=1, source_target_pairs={{0,13},{4,1},{8,5},{12,9},{16,29},{20,17},{24,21},{28,25}} | collective-permute-start | bytes 98312 | tf_op jit(solution)/shard_map/ppermute | solution.py:57
  43.1 0.0 collective-permute-done.refs_1_.own
  43.1 0.3 collective-permute-done.2.refs_3_
  43.4 1.3 %collective-permute-done.3.refs_4_ = bf16[8,2048]{1,0:T(8,128)(2,1)S(1)} collective-permute-done((bf16[8,2048]{1,0:T(8,128)(2,1)S(1)}, bf16[8,2048]{1,0:T(8,128)(2,1)S(1)}, u32[]{:S(2)}, u32[]{:S(2)}) %collective-permute-start.3) | collective-permute-done | bytes 32800 | tf_op jit(solution)/shard_map/ppermute | solution.py:57
  44.7 2.0 %shard_map.95 = f32[4,8,640]{2,1,0:T(8,128)S(1)} custom-call(s32[4]{0:T(128)S(1)} %and_select_fusion.sources, bf16[1,8192]{1,0:T(2,128)(2,1)S(1)} %copy-done.5, bf16[8192,128]{1,0:T(8,128)(2,1)S(1)} %bitcast.12, bf16[8192,256]{1,0:T(8,128)(2,1)S(1)} %bitcast.8, bf16[1,128]{1,0:T(2,128)(2,1)S(1)} %copy-done.9, f32[4,8,96]{2,1,0:T(8,128)S(1)} %get-tuple-element.15.counts, ...), custom_call_target="tpu_custom_call" | custom-call | tf_op jit(solution)/shard_map/pallas_call | solution.py:35
  46.7 8.3 %all_to_all.26.slots = f32[4,8,640]{2,1,0:T(8,128)S(1)} all-to-all(f32[4,8,640]{2,1,0:T(8,128)S(1)} %shard_map.95), channel_id=1, replica_groups=mesh['groups'=2,'tensor'=4,'section'=4] {'tensor'}, dimensions={0} | all-to-all | bytes 163840 | tf_op jit(solution)/shard_map/all_to_all | solution.py:67
  55.0 0.5 shard_map.96
  55.5 0.7 collective-permute-start.4
  56.2 0.7 collective-permute-start.5
  56.9 0.7 collective-permute-start.6
  57.5 0.7 collective-permute-start.7
  58.2 0.0 collective-permute-done.4.refs_1_.own
  58.2 0.0 collective-permute-done.6.refs_3_
  58.3 2.0 %shard_map.97 = f32[4,8,640]{2,1,0:T(8,128)S(1)} custom-call(s32[4]{0:T(128)S(1)} %and_select_fusion.sources, bf16[1,8192]{1,0:T(2,128)(2,1)S(1)} %copy-done.5, bf16[8192,128]{1,0:T(8,128)(2,1)S(1)} %bitcast.13, bf16[8192,256]{1,0:T(8,128)(2,1)S(1)} %bitcast.9, bf16[1,128]{1,0:T(2,128)(2,1)S(1)} %copy-done.9, f32[4,8,96]{2,1,0:T(8,128)S(1)} %get-tuple-element.15.counts, ...), custom_call_target="tpu_custom_call" | custom-call | tf_op jit(solution)/shard_map/pallas_call | solution.py:35
  60.3 8.2 %all_to_all.27.slots = f32[4,8,640]{2,1,0:T(8,128)S(1)} all-to-all(f32[4,8,640]{2,1,0:T(8,128)S(1)} %shard_map.97), channel_id=1, replica_groups=mesh['groups'=2,'tensor'=4,'section'=4] {'tensor'}, dimensions={0} | all-to-all | bytes 163840 | tf_op jit(solution)/shard_map/all_to_all | solution.py:67
  68.4 0.5 shard_map.98
  68.9 0.7 collective-permute-start.10
  69.6 0.7 collective-permute-start.11
  70.3 0.7 collective-permute-start.8
  71.0 0.7 collective-permute-start.9
  71.7 2.0 %shard_map.99 = f32[4,8,640]{2,1,0:T(8,128)S(1)} custom-call(s32[4]{0:T(128)S(1)} %and_select_fusion.sources, bf16[1,8192]{1,0:T(2,128)(2,1)S(1)} %copy-done.5, bf16[8192,128]{1,0:T(8,128)(2,1)S(1)} %bitcast.14, bf16[8192,256]{1,0:T(8,128)(2,1)S(1)} %bitcast.10, bf16[1,128]{1,0:T(2,128)(2,1)S(1)} %copy-done.9, f32[4,8,96]{2,1,0:T(8,128)S(1)} %get-tuple-element.15.counts, ...), custom_call_target="tpu_custom_call" | custom-call | tf_op jit(solution)/shard_map/pallas_call | solution.py:35
  73.7 8.2 %all_to_all.28.slots = f32[4,8,640]{2,1,0:T(8,128)S(1)} all-to-all(f32[4,8,640]{2,1,0:T(8,128)S(1)} %shard_map.99), channel_id=1, replica_groups=mesh['groups'=2,'tensor'=4,'section'=4] {'tensor'}, dimensions={0} | all-to-all | bytes 163840 | tf_op jit(solution)/shard_map/all_to_all | solution.py:67
  81.8 0.5 shard_map.100
  82.3 1.3 %collective-permute-start.12 = (bf16[2,2048]{1,0:T(2,128)(2,1)S(1)}, bf16[2,2048]{1,0:T(2,128)(2,1)S(1)}, u32[]{:S(2)}, u32[]{:S(2)}) collective-permute-start(bf16[2,2048]{1,0:T(2,128)(2,1)S(1)} %get-tuple-element.18), channel_id=1, source_target_pairs={{3,0},{7,4},{11,8},{15,12},{19,16},{23,20},{27,24},{31,28}} | collective-permute-start | bytes 24584 | tf_op jit(solution)/shard_map/ppermute | solution.py:310
  83.6 0.7 collective-permute-start.13
  84.3 0.7 collective-permute-start.14
  85.0 12.6 %collective-permute-done.12 = bf16[2,2048]{1,0:T(2,128)(2,1)S(1)} collective-permute-done((bf16[2,2048]{1,0:T(2,128)(2,1)S(1)}, bf16[2,2048]{1,0:T(2,128)(2,1)S(1)}, u32[]{:S(2)}, u32[]{:S(2)}) %collective-permute-start.12) | collective-permute-done | bytes 8224 | tf_op jit(solution)/shard_map/ppermute | solution.py:310
  97.6 0.6 fusion.2
  (26 shorter events, 0.1 us)
Async XLA Ops:
  0.0 0.9 copy-start.6
  0.9 0.8 copy-start.7
  1.7 0.7 copy-start.10
  2.4 0.7 copy-start.11
  4.4 17.3 %all-to-all-start = ((bf16[4,176,256]{2,1,0:T(8,128)(2,1)}), bf16[4,176,256]{2,1,0:T(8,128)(2,1)S(1)}, u32[]{:S(2)}, u32[]{:S(2)}) async-start(bf16[4,176,256]{2,1,0:T(8,128)(2,1)} %shard_map.91), calls=%async_computation | async-start | bytes 720896 | tf_op jit(solution)/shard_map/all_to_all | solution.py:67
  21.7 2.2 %copy-start = (bf16[1,8192,256]{2,1,0:T(8,128)(2,1)S(1)}, bf16[1,8192,256]{2,1,0:T(8,128)(2,1)}, u32[]{:S(2)}) copy-start(bf16[1,8192,256]{2,1,0:T(8,128)(2,1)} %param.13) | copy-start | bytes 12582916
  23.9 1.6 %copy-start.2 = (bf16[1,8192,128]{2,1,0:T(8,128)(2,1)S(1)}, bf16[1,8192,128]{2,1,0:T(8,128)(2,1)}, u32[]{:S(2)}) copy-start(bf16[1,8192,128]{2,1,0:T(8,128)(2,1)} %param.11) | copy-start | bytes 6291460
  25.5 0.8 copy-start.5
  26.3 0.7 copy-start.9
  26.9 10.4 %copy-start.4 = (bf16[1,512,2048]{2,1,0:T(8,128)(2,1)S(1)}, bf16[1,512,2048]{2,1,0:T(8,128)(2,1)}, u32[]{:S(2)}) copy-start(bf16[1,512,2048]{2,1,0:T(8,128)(2,1)} %param.14) | copy-start | bytes 6291460
  26.9 10.4 %copy-start.8 = (bf16[8,2048]{1,0:T(8,128)(2,1)S(1)}, bf16[8,2048]{1,0:T(8,128)(2,1)}, u32[]{:S(2)}) copy-start(bf16[8,2048]{1,0:T(8,128)(2,1)} %own.1) | copy-start | bytes 98308
  26.9 17.7 %copy-start.1 = (bf16[1,8192,256]{2,1,0:T(8,128)(2,1)S(1)}, bf16[1,8192,256]{2,1,0:T(8,128)(2,1)}, u32[]{:S(2)}) copy-start(bf16[1,8192,256]{2,1,0:T(8,128)(2,1)} %param.13) | copy-start | bytes 12582916
  28.9 15.8 %copy-start.3 = (bf16[1,8192,128]{2,1,0:T(8,128)(2,1)S(1)}, bf16[1,8192,128]{2,1,0:T(8,128)(2,1)}, u32[]{:S(2)}) copy-start(bf16[1,8192,128]{2,1,0:T(8,128)(2,1)} %param.11) | copy-start | bytes 6291460
  37.9 5.2 %collective-permute-start = (bf16[8,2048]{1,0:T(8,128)(2,1)S(1)}, bf16[8,2048]{1,0:T(8,128)(2,1)S(1)}, u32[]{:S(2)}, u32[]{:S(2)}) collective-permute-start(bf16[8,2048]{1,0:T(8,128)(2,1)S(1)} %shard_map.94), channel_id=1, source_target_pairs={{0,1},{4,5},{8,9},{12,13},{16,17},{20,21},{24,25},{28,29}} | collective-permute-start | bytes 98312 | tf_op jit(solution)/shard_map/ppermute | solution.py:57
  39.2 3.9 %collective-permute-start.1 = (bf16[8,2048]{1,0:T(8,128)(2,1)S(1)}, bf16[8,2048]{1,0:T(8,128)(2,1)S(1)}, u32[]{:S(2)}, u32[]{:S(2)}) collective-permute-start(bf16[8,2048]{1,0:T(8,128)(2,1)S(1)} %shard_map.94), channel_id=1, source_target_pairs={{0,5},{4,9},{8,13},{12,1},{16,21},{20,25},{24,29},{28,17}} | collective-permute-start | bytes 98312 | tf_op jit(solution)/shard_map/ppermute | solution.py:57
  40.5 2.9 %collective-permute-start.2 = (bf16[8,2048]{1,0:T(8,128)(2,1)S(1)}, bf16[8,2048]{1,0:T(8,128)(2,1)S(1)}, u32[]{:S(2)}, u32[]{:S(2)}) collective-permute-start(bf16[8,2048]{1,0:T(8,128)(2,1)S(1)} %shard_map.94), channel_id=1, source_target_pairs={{0,9},{4,13},{8,1},{12,5},{16,25},{20,29},{24,17},{28,21}} | collective-permute-start | bytes 98312 | tf_op jit(solution)/shard_map/ppermute | solution.py:57
  41.8 2.9 %collective-permute-start.3 = (bf16[8,2048]{1,0:T(8,128)(2,1)S(1)}, bf16[8,2048]{1,0:T(8,128)(2,1)S(1)}, u32[]{:S(2)}, u32[]{:S(2)}) collective-permute-start(bf16[8,2048]{1,0:T(8,128)(2,1)S(1)} %shard_map.94), channel_id=1, source_target_pairs={{0,13},{4,1},{8,5},{12,9},{16,29},{20,17},{24,21},{28,25}} | collective-permute-start | bytes 98312 | tf_op jit(solution)/shard_map/ppermute | solution.py:57
  55.5 2.7 %collective-permute-start.4 = (bf16[8,2048]{1,0:T(8,128)(2,1)S(1)}, bf16[8,2048]{1,0:T(8,128)(2,1)S(1)}, u32[]{:S(2)}, u32[]{:S(2)}) collective-permute-start(bf16[8,2048]{1,0:T(8,128)(2,1)S(1)} %shard_map.96), channel_id=1, source_target_pairs={{1,2},{5,6},{9,10},{13,14},{17,18},{21,22},{25,26},{29,30}} | collective-permute-start | bytes 98312 | tf_op jit(solution)/shard_map/ppermute | solution.py:57
  56.2 2.0 %collective-permute-start.5 = (bf16[8,2048]{1,0:T(8,128)(2,1)S(1)}, bf16[8,2048]{1,0:T(8,128)(2,1)S(1)}, u32[]{:S(2)}, u32[]{:S(2)}) collective-permute-start(bf16[8,2048]{1,0:T(8,128)(2,1)S(1)} %shard_map.96), channel_id=1, source_target_pairs={{1,6},{5,10},{9,14},{13,2},{17,22},{21,26},{25,30},{29,18}} | collective-permute-start | bytes 98312 | tf_op jit(solution)/shard_map/ppermute | solution.py:57
  56.9 1.4 %collective-permute-start.6 = (bf16[8,2048]{1,0:T(8,128)(2,1)S(1)}, bf16[8,2048]{1,0:T(8,128)(2,1)S(1)}, u32[]{:S(2)}, u32[]{:S(2)}) collective-permute-start(bf16[8,2048]{1,0:T(8,128)(2,1)S(1)} %shard_map.96), channel_id=1, source_target_pairs={{1,10},{5,14},{9,2},{13,6},{17,26},{21,30},{25,18},{29,22}} | collective-permute-start | bytes 98312 | tf_op jit(solution)/shard_map/ppermute | solution.py:57
  57.5 0.7 collective-permute-start.7
  68.9 2.7 %collective-permute-start.10 = (bf16[8,2048]{1,0:T(8,128)(2,1)S(1)}, bf16[8,2048]{1,0:T(8,128)(2,1)S(1)}, u32[]{:S(2)}, u32[]{:S(2)}) collective-permute-start(bf16[8,2048]{1,0:T(8,128)(2,1)S(1)} %shard_map.98), channel_id=1, source_target_pairs={{2,11},{6,15},{10,3},{14,7},{18,27},{22,31},{26,19},{30,23}} | collective-permute-start | bytes 98312 | tf_op jit(solution)/shard_map/ppermute | solution.py:57
  69.6 2.0 %collective-permute-start.11 = (bf16[8,2048]{1,0:T(8,128)(2,1)S(1)}, bf16[8,2048]{1,0:T(8,128)(2,1)S(1)}, u32[]{:S(2)}, u32[]{:S(2)}) collective-permute-start(bf16[8,2048]{1,0:T(8,128)(2,1)S(1)} %shard_map.98), channel_id=1, source_target_pairs={{2,15},{6,3},{10,7},{14,11},{18,31},{22,19},{26,23},{30,27}} | collective-permute-start | bytes 98312 | tf_op jit(solution)/shard_map/ppermute | solution.py:57
  70.3 1.4 %collective-permute-start.8 = (bf16[8,2048]{1,0:T(8,128)(2,1)S(1)}, bf16[8,2048]{1,0:T(8,128)(2,1)S(1)}, u32[]{:S(2)}, u32[]{:S(2)}) collective-permute-start(bf16[8,2048]{1,0:T(8,128)(2,1)S(1)} %shard_map.98), channel_id=1, source_target_pairs={{2,3},{6,7},{10,11},{14,15},{18,19},{22,23},{26,27},{30,31}} | collective-permute-start | bytes 98312 | tf_op jit(solution)/shard_map/ppermute | solution.py:57
  71.0 0.7 collective-permute-start.9
  82.3 15.2 %collective-permute-start.12 = (bf16[2,2048]{1,0:T(2,128)(2,1)S(1)}, bf16[2,2048]{1,0:T(2,128)(2,1)S(1)}, u32[]{:S(2)}, u32[]{:S(2)}) collective-permute-start(bf16[2,2048]{1,0:T(2,128)(2,1)S(1)} %get-tuple-element.18), channel_id=1, source_target_pairs={{3,0},{7,4},{11,8},{15,12},{19,16},{23,20},{27,24},{31,28}} | collective-permute-start | bytes 24584 | tf_op jit(solution)/shard_map/ppermute | solution.py:310
  83.6 13.9 %collective-permute-start.13 = (bf16[2,2048]{1,0:T(2,128)(2,1)S(1)}, bf16[2,2048]{1,0:T(2,128)(2,1)S(1)}, u32[]{:S(2)}, u32[]{:S(2)}) collective-permute-start(bf16[2,2048]{1,0:T(2,128)(2,1)S(1)} %get-tuple-element.19), channel_id=1, source_target_pairs={{3,1},{7,5},{11,9},{15,13},{19,17},{23,21},{27,25},{31,29}} | collective-permute-start | bytes 24584 | tf_op jit(solution)/shard_map/ppermute | solution.py:310
  84.3 13.3 %collective-permute-start.14 = (bf16[2,2048]{1,0:T(2,128)(2,1)S(1)}, bf16[2,2048]{1,0:T(2,128)(2,1)S(1)}, u32[]{:S(2)}, u32[]{:S(2)}) collective-permute-start(bf16[2,2048]{1,0:T(2,128)(2,1)S(1)} %get-tuple-element.20), channel_id=1, source_target_pairs={{3,2},{7,6},{11,10},{15,14},{19,18},{23,22},{27,26},{31,30}} | collective-permute-start | bytes 24584 | tf_op jit(solution)/shard_map/ppermute | solution.py:310

commit v3 on v2

--- a/solution.py
+++ b/solution.py
@@ -2,6 +2,7 @@
 
 import jax
 import jax.numpy as jnp
+import numpy as np
 from jax import lax
 from jax.experimental import pallas as pl
 from jax.experimental.pallas import tpu as pltpu
@@ -20,7 +21,7 @@
     return -(-value // unit) * unit
 
 
-def kernel_call(body, outs, in_specs, scratch=(), many=True):
+def kernel_call(body, outs, in_specs, scratch=(), many=True, place=True):
     specs = [VMEM] * len(outs)
     call = pl.pallas_call(
         body,
@@ -32,9 +33,12 @@
     )
 
     def placed(*operands):
+        put = pltpu.with_memory_space_constraint
+        if not place:
+            return call(*[put(value, pltpu.HBM) for value in operands])
         return call(
             *[
-                pltpu.with_memory_space_constraint(value, pltpu.VMEM) if spec is VMEM else value
+                put(value, pltpu.VMEM) if spec is VMEM else value
                 for value, spec in zip(operands, in_specs)
             ]
         )
@@ -47,9 +51,6 @@
         self.count = lax.axis_size("tensor")
         self.sections = lax.axis_size("section")
         self.direct = self.count <= DIRECT_PEERS
-        me = lax.axis_index("tensor")
-        order = jnp.arange(self.count, dtype=jnp.int32)
-        self.sources = (me - order) % self.count if self.direct else order
 
     def send(self, value, origin, target, step):
         n, m = self.count, self.sections
@@ -60,11 +61,34 @@
         if self.direct:
             return [self.send(value, origin, target, step) for step in range(self.count)]
         value = lax.ppermute(value, "section", [(origin, target)])
-        whole = lax.all_gather(value, "tensor", axis=0, tiled=False)
-        return [whole[slot] for slot in range(self.count)]
+        return [lax.all_gather(value, "tensor", axis=1, tiled=True)]
 
     def trade(self, values):
         return lax.all_to_all(values, "tensor", split_axis=0, concat_axis=0, tiled=True)
+
+
+def load_kernel(*refs):
+    count = len(refs) // 2 - 1
+    sources, outs, arrived = refs[:count], refs[count + 1 : -1], refs[-1]
+    copies = [
+        pltpu.make_async_copy(sources[i], outs[i], arrived.at[i]) for i in range(count)
+    ]
+    for copy in copies:
+        copy.start()
+    for copy in copies:
+        copy.wait()
+
+
+def load(values, after):
+    hbm = pl.BlockSpec(memory_space=pltpu.HBM)
+    return pl.pallas_call(
+        load_kernel,
+        out_shape=[pltpu.VMEM(value.shape, value.dtype) for value in values],
+        in_specs=[hbm] * (len(values) + 1),
+        out_specs=[VMEM] * len(values),
+        scratch_shapes=[pltpu.SemaphoreType.DMA((len(values),))],
+        compiler_params=pltpu.CompilerParams(vmem_limit_bytes=KERNEL_VMEM),
+    )(*[pltpu.with_memory_space_constraint(value, pltpu.HBM) for value in values], after)
 
 
 def pack_kernel(info, tensor_ref, table, context, pool, hidden, out):
@@ -127,14 +151,15 @@
     return values * cosine + swapped * sine
 
 
-def project_kernel(info, sources, gain, wq, wkv, bias, counts, cosine, sine, *refs):
-    n, heads_dev, group, tokens, width = info
+def project_kernel(info, tensor_ref, gain, wq, wkv, bias, counts, cosine, sine, *refs):
+    n, heads_dev, group, tokens, width, rotated_order = info
     packs, *pieces, out = refs
     features = gain.shape[1]
     slice_len = features // n
-    if len(pieces) == n:
+    if rotated_order:
         wide = [piece[...].astype(jnp.float32) for piece in pieces]
-        starts = [pl.multiple_of(sources[k] * slice_len, HD) for k in range(n)]
+        me = tensor_ref[0]
+        starts = [pl.multiple_of((me + n - k) % n * slice_len, HD) for k in range(n)]
     else:
         starts = [k * slice_len for k in range(n)]
         wide = [pieces[0][:, at : at + slice_len].astype(jnp.float32) for at in starts]
@@ -153,7 +178,7 @@
         fresh = kv_part if k == 0 else fresh + kv_part
     queries = (queries + bias[...].astype(jnp.float32)).astype(jnp.bfloat16).astype(jnp.float32)
     span = heads_dev * HD
-    out[0, :, 3 * span : 3 * span + fresh.shape[1]] = fresh.astype(jnp.bfloat16).astype(jnp.float32)
+    out[0, :, 3 * span : 3 * span + fresh.shape[1]] = fresh.astype(jnp.bfloat16)
     for i in range(heads_dev):
         head = slice(i * HD, (i + 1) * HD)
         rotated = rotate(queries[:, head], cosine[...], sine[...]).astype(jnp.bfloat16)
@@ -182,11 +207,18 @@
             mixed = mixed + jnp.dot(
                 weight.astype(jnp.bfloat16), values, preferred_element_type=jnp.float32
             )
-        out[0, :, i * HD : (i + 1) * HD] = rotated.astype(jnp.float32)
-        out[0, :, span + i * HD : span + (i + 1) * HD] = mixed / mass
-        out[0, :, 2 * span + i * HD : 2 * span + (i + 1) * HD] = jnp.broadcast_to(
-            top + jnp.log(mass), (mixed.shape[0], HD)
+        out[0, :, i * HD : (i + 1) * HD] = rotated
+        out[0, :, span + i * HD : span + (i + 1) * HD] = (mixed / mass).astype(
+            jnp.bfloat16
         )
+        level = jnp.broadcast_to(top + jnp.log(mass), (mixed.shape[0], HD))
+        lane = lax.broadcasted_iota(jnp.int32, level.shape, 1)
+        upper = level.astype(jnp.bfloat16).astype(jnp.float32)
+        middle = (level - upper).astype(jnp.bfloat16).astype(jnp.float32)
+        lower = level - upper - middle
+        terms = jnp.where(lane == 0, upper, jnp.where(lane == 1, middle, lower))
+        terms = jnp.where(lane < 3, terms, 0.0).astype(jnp.bfloat16)
+        out[0, :, 2 * span + i * HD : 2 * span + (i + 1) * HD] = terms
     for k in range(1, n):
         out[k] = out[0]
 
@@ -197,7 +229,9 @@
     fresh = refs[splits]
     span = heads_dev * HD
     for j in range(n):
-        fresh[:, j * kv_width : (j + 1) * kv_width] = slots[j, :, 3 * span : 3 * span + kv_width]
+        fresh[:, j * kv_width : (j + 1) * kv_width] = slots[
+            j, :, 3 * span : 3 * span + kv_width
+        ].astype(jnp.float32)
     keys = []
     for h in range(kv_heads):
         key = rotate(fresh[:, h * HD : (h + 1) * HD], cosine[...], sine[...])
@@ -206,9 +240,10 @@
     for h in range(n * heads_dev):
         j, i = divmod(h, heads_dev)
         kv = h // group
-        query = slots[j, :, i * HD : (i + 1) * HD]
-        cached = slots[j, :, span + i * HD : span + (i + 1) * HD]
-        level = slots[j, :, 2 * span + i * HD : 2 * span + (i + 1) * HD]
+        query = slots[j, :, i * HD : (i + 1) * HD].astype(jnp.float32)
+        cached = slots[j, :, span + i * HD : span + (i + 1) * HD].astype(jnp.float32)
+        terms = slots[j, :, 2 * span + i * HD : 2 * span + (i + 1) * HD]
+        level = jnp.sum(terms.astype(jnp.float32), axis=1, keepdims=True)
         value = fresh[:, (kv_heads + kv) * HD : (kv_heads + kv + 1) * HD]
         score = jnp.sum(query * keys[kv], axis=1, keepdims=True) * HD ** (-0.5)
         weight = 1.0 / (1.0 + jnp.exp(level - score))
@@ -259,6 +294,7 @@
         [jax.ShapeDtypeStruct((n, height, 2 * width), bf16)],
         [SMEM] * 3 + [VMEM] * 2,
         many=False,
+        place=False,
     )(
         tensor_id.reshape(1),
         page_table,
@@ -266,9 +302,10 @@
         kv_pool.reshape(tokens, kv_pool.shape[3]),
         hidden,
     )
+    wout, gain, bias = load((wout, norm_gain, query_bias), packs)
     packs = ring.trade(packs)
-    frequency = rope_base ** (-(jnp.arange(HD // 2, dtype=f32) * 2.0) / HD)
-    frequency = jnp.concatenate([frequency, frequency])[None, :]
+    frequency = np.float32(rope_base) ** (-(np.arange(HD // 2, dtype=np.float32) * 2.0) / HD)
+    frequency = np.concatenate([frequency, frequency])[None, :].astype(np.float32)
     counts, cosine, sine, first = kernel_call(
         functools.partial(unpack_kernel, (n, row_dev, tokens, extra)),
         [
@@ -282,15 +319,16 @@
     )(frequency, packs)
 
     message = 3 * heads_dev * HD + round_up(kv_width, HD)
+    project_info = (n, heads_dev, group, tokens, width)
     pieces = [first]
     own = hidden
     for layer in range(sections):
         sent = kernel_call(
-            functools.partial(project_kernel, (n, heads_dev, group, tokens, width)),
-            [jax.ShapeDtypeStruct((n, rows, message), f32)],
+            functools.partial(project_kernel, project_info + (ring.direct and layer > 0,)),
+            [jax.ShapeDtypeStruct((n, rows, message), bf16)],
             [SMEM] + [VMEM] * (8 + len(pieces)),
             many=False,
-        )(ring.sources, norm_gain, wq, wkv, query_bias, counts, cosine, sine, packs, *pieces)
+        )(tensor_id.reshape(1), gain, wq, wkv, bias, counts, cosine, sine, packs, *pieces)
         parts = ring.trade(sent)
         splits = sections if layer == sections - 1 else 1
         stream = kernel_call(
@@ -303,7 +341,7 @@
         )(own, wout, cosine, sine, parts)
         if layer < sections - 1:
             pieces = ring.advance(stream[0], layer, layer + 1)
-            own = pieces[0] if ring.direct else pieces_own(pieces, tensor_id)
+            own = pieces[0] if ring.direct else own_slice(pieces[0], tensor_id, slice_len)
     last = sections - 1
     result = jnp.where(section_id == last, stream[last], jnp.zeros_like(stream[last]))
     for target in range(last):
@@ -311,8 +349,8 @@
     return result
 
 
-def pieces_own(pieces, tensor_id):
-    return lax.dynamic_index_in_dim(jnp.stack(pieces), tensor_id, 0, keepdims=False)
+def own_slice(whole, tensor_id, slice_len):
+    return lax.dynamic_slice_in_dim(whole, tensor_id * slice_len, slice_len, axis=1)
 
 
 def solution(mesh):

time: 99.6 us -> 94.3 us (0.947)
  local copies, waits for them, and re-layouts: 8.22 us -> 3.52 us
    unnamed x24 -> x14, local copies, waits for them, and re-layouts: 8.22 us -> 3.52 us
    ppermute x3, waiting for transfers between devices: 12.6 us -> 16.1 us  [shards(): result = result + lax.ppermute(stream[target], 'section', [(last, target)])]
    all_to_all x1, waiting for transfers between devices: 10.9 us -> 8.02 us  [trade(): lax.all_to_all(values, 'tensor', split_axis=0, concat_axis=0, tiled=True)]
    pallas_call x10 -> x11, Pallas kernels: 11.4 us -> 11.5 us  [the longest x9 7.97 us: placed(): call(*[put(value, pltpu.VMEM) if spec is VMEM else value for value, spec...]
  transfers between devices with their start and end apart: 16 -> 16, of which waited for: 4 -> 4; matrix products, arithmetic and copies ran while one was open for 0% -> 0% of each run, Pallas kernels for 0% -> 2%
where the time goes in v3:
time: 94.3 us; the launch traced here: 93.7 us
  blocking collectives  32.6 us (35%)
  waiting for transfers between devices  25.7 us (27%)
  starting transfers between devices  19.5 us (21%)
  Pallas kernels  11.5 us (12%)
  local copies, waits for them, and re-layouts  3.52 us (4%)
    all_to_all x4, blocking collectives, trade(): lax.all_to_all(values, 'tensor', split_axis=0, concat_axis=0, tiled=True)  32.6 us
    ppermute x3, waiting for transfers between devices, shards(): result = result + lax.ppermute(stream[target], 'section', [(last, target)])  16.1 us
    ppermute x12, starting transfers between devices, send(): return lax.ppermute(value, ('tensor', 'section'), perm)  10.5 us
    all_to_all x1, waiting for transfers between devices, trade(): lax.all_to_all(values, 'tensor', split_axis=0, concat_axis=0, tiled=True)  8.02 us
    pallas_call x9, Pallas kernels, placed(): call(*[put(value, pltpu.VMEM) if spec is VMEM else value for value, spec...  7.97 us
    all_to_all x1, starting transfers between devices, trade(): lax.all_to_all(values, 'tensor', split_axis=0, concat_axis=0, tiled=True)  6.35 us
    unnamed x14, local copies, waits for them, and re-layouts  3.52 us
    ppermute x3, starting transfers between devices, shards(): result = result + lax.ppermute(stream[target], 'section', [(last, target)])  2.63 us
  transfers between devices with their start and end apart: 16, of which 4 were waited for; matrix products, arithmetic and copies ran while one was open for 0% of the time, Pallas kernels for 2%

profile of v3, /device:TPU:0, one launch (start us, length us, event | category | flops | bytes accessed | tf_op | source)
XLA Modules:
  0.0 93.7 jit_solution(15166067827963776223)
XLA Ops:
  0.0 1.9 %shard_map.100.refs_3_ = bf16[4,176,256]{2,1,0:T(8,128)(2,1)} custom-call(s32[1]{0:T(128)} %bitcast.1.tensor_ref, s32[2,4]{1,0:T(2,128)} %table.1, s32[2]{0:T(128)} %context.1, bf16[96,1024]{1,0:T(8,128)(2,1)} %bitcast.14, bf16[8,2048]{1,0:T(8,128)(2,1)} %own.1), custom_call_target="tpu_custom_call" | custom-call | tf_op jit(solution)/shard_map/pallas_call | solution.py:38
  1.9 6.3 %all-to-all-start = ((bf16[4,176,256]{2,1,0:T(8,128)(2,1)}), bf16[4,176,256]{2,1,0:T(8,128)(2,1)S(1)}, u32[]{:S(2)}, u32[]{:S(2)}) async-start(bf16[4,176,256]{2,1,0:T(8,128)(2,1)} %shard_map.100.refs_3_), calls=%async_computation | async-start | bytes 720896 | tf_op jit(solution)/shard_map/all_to_all | solution.py:67
  8.2 1.6 %shard_map.101 = (bf16[512,2048]{1,0:T(8,128)(2,1)S(1)}, bf16[1,8192]{1,0:T(2,128)(2,1)S(1)}, bf16[1,128]{1,0:T(2,128)(2,1)S(1)}) custom-call(bf16[512,2048]{1,0:T(8,128)(2,1)} %bitcast.13, bf16[1,8192]{1,0:T(2,128)(2,1)} %refs_1_.1, bf16[1,128]{1,0:T(2,128)(2,1)} %refs_2_.1, bf16[4,176,256]{2,1,0:T(8,128)(2,1)} %shard_map.100.refs_3_), custom_call_target="tpu_custom_call" | custom-call | tf_op jit(solution)/shard_map/pallas_call | solution.py:84
  9.9 1.3 %copy-done.3 = bf16[512,2048]{1,0:T(8,128)(2,1)} copy-done((bf16[512,2048]{1,0:T(8,128)(2,1)}, bf16[512,2048]{1,0:T(8,128)(2,1)S(1)}, u32[]{:S(2)}) %copy-start.3) | copy-done | bytes 2097176
  11.2 8.0 %all-to-all-done.packs.refs_0_ = bf16[4,176,256]{2,1,0:T(8,128)(2,1)S(1)} async-done(((bf16[4,176,256]{2,1,0:T(8,128)(2,1)}), bf16[4,176,256]{2,1,0:T(8,128)(2,1)S(1)}, u32[]{:S(2)}, u32[]{:S(2)}) %all-to-all-start) | async-done | bytes 360480 | tf_op jit(solution)/shard_map/all_to_all | solution.py:67
  19.2 0.1 shard_map.102
  19.3 0.0 copy-start
  19.3 2.2 %copy-done = bf16[1,8192,256]{2,1,0:T(8,128)(2,1)S(1)} copy-done((bf16[1,8192,256]{2,1,0:T(8,128)(2,1)S(1)}, bf16[1,8192,256]{2,1,0:T(8,128)(2,1)}, u32[]{:S(2)}) %copy-start) | copy-done | bytes 4194328
  21.5 1.4 %shard_map.103 = bf16[4,8,640]{2,1,0:T(8,128)(2,1)S(1)} custom-call(s32[1]{0:T(128)} %bitcast.1.tensor_ref, bf16[1,8192]{1,0:T(2,128)(2,1)S(1)} %get-tuple-element.19.gain, bf16[8192,128]{1,0:T(8,128)(2,1)S(1)} %bitcast.9, bf16[8192,256]{1,0:T(8,128)(2,1)S(1)} %bitcast.5, bf16[1,128]{1,0:T(2,128)(2,1)S(1)} %get-tuple-element.20.bias, ...), custom_call_target="tpu_custom_call" | custom-call | tf_op jit(solution)/shard_map/pallas_call | solution.py:39
  22.9 8.3 %all_to_all.25.slots = bf16[4,8,640]{2,1,0:T(8,128)(2,1)S(1)} all-to-all(bf16[4,8,640]{2,1,0:T(8,128)(2,1)S(1)} %shard_map.103), channel_id=1, replica_groups=mesh['groups'=2,'tensor'=4,'section'=4] {'tensor'}, dimensions={0} | all-to-all | bytes 81920 | tf_op jit(solution)/shard_map/all_to_all | solution.py:67
  31.3 0.5 shard_map.104
  31.8 1.3 %collective-permute-start = (bf16[8,2048]{1,0:T(8,128)(2,1)S(1)}, bf16[8,2048]{1,0:T(8,128)(2,1)S(1)}, u32[]{:S(2)}, u32[]{:S(2)}) collective-permute-start(bf16[8,2048]{1,0:T(8,128)(2,1)S(1)} %shard_map.104), channel_id=1, source_target_pairs={{0,1},{4,5},{8,9},{12,13},{16,17},{20,21},{24,25},{28,29}} | collective-permute-start | bytes 98312 | tf_op jit(solution)/shard_map/ppermute | solution.py:58
  33.1 1.3 %collective-permute-start.1 = (bf16[8,2048]{1,0:T(8,128)(2,1)S(1)}, bf16[8,2048]{1,0:T(8,128)(2,1)S(1)}, u32[]{:S(2)}, u32[]{:S(2)}) collective-permute-start(bf16[8,2048]{1,0:T(8,128)(2,1)S(1)} %shard_map.104), channel_id=1, source_target_pairs={{0,5},{4,9},{8,13},{12,1},{16,21},{20,25},{24,29},{28,17}} | collective-permute-start | bytes 98312 | tf_op jit(solution)/shard_map/ppermute | solution.py:58
  34.4 1.3 %collective-permute-start.2 = (bf16[8,2048]{1,0:T(8,128)(2,1)S(1)}, bf16[8,2048]{1,0:T(8,128)(2,1)S(1)}, u32[]{:S(2)}, u32[]{:S(2)}) collective-permute-start(bf16[8,2048]{1,0:T(8,128)(2,1)S(1)} %shard_map.104), channel_id=1, source_target_pairs={{0,9},{4,13},{8,1},{12,5},{16,25},{20,29},{24,17},{28,21}} | collective-permute-start | bytes 98312 | tf_op jit(solution)/shard_map/ppermute | solution.py:58
  35.7 1.3 %collective-permute-start.3 = (bf16[8,2048]{1,0:T(8,128)(2,1)S(1)}, bf16[8,2048]{1,0:T(8,128)(2,1)S(1)}, u32[]{:S(2)}, u32[]{:S(2)}) collective-permute-start(bf16[8,2048]{1,0:T(8,128)(2,1)S(1)} %shard_map.104), channel_id=1, source_target_pairs={{0,13},{4,1},{8,5},{12,9},{16,29},{20,17},{24,21},{28,25}} | collective-permute-start | bytes 98312 | tf_op jit(solution)/shard_map/ppermute | solution.py:58
  37.0 0.0 collective-permute-done.refs_1_.own
  37.0 0.0 collective-permute-done.1.refs_2_
  37.0 0.3 collective-permute-done.2.refs_3_
  37.3 1.3 %collective-permute-done.3.refs_4_ = bf16[8,2048]{1,0:T(8,128)(2,1)S(1)} collective-permute-done((bf16[8,2048]{1,0:T(8,128)(2,1)S(1)}, bf16[8,2048]{1,0:T(8,128)(2,1)S(1)}, u32[]{:S(2)}, u32[]{:S(2)}) %collective-permute-start.3) | collective-permute-done | bytes 32800 | tf_op jit(solution)/shard_map/ppermute | solution.py:58
  38.6 1.5 %shard_map.105 = bf16[4,8,640]{2,1,0:T(8,128)(2,1)S(1)} custom-call(s32[1]{0:T(128)} %bitcast.1.tensor_ref, bf16[1,8192]{1,0:T(2,128)(2,1)S(1)} %get-tuple-element.19.gain, bf16[8192,128]{1,0:T(8,128)(2,1)S(1)} %bitcast.10, bf16[8192,256]{1,0:T(8,128)(2,1)S(1)} %bitcast.6, bf16[1,128]{1,0:T(2,128)(2,1)S(1)} %get-tuple-element.20.bias, ...), custom_call_target="tpu_custom_call" | custom-call | tf_op jit(solution)/shard_map/pallas_call | solution.py:39
  40.1 8.2 %all_to_all.26.slots = bf16[4,8,640]{2,1,0:T(8,128)(2,1)S(1)} all-to-all(bf16[4,8,640]{2,1,0:T(8,128)(2,1)S(1)} %shard_map.105), channel_id=1, replica_groups=mesh['groups'=2,'tensor'=4,'section'=4] {'tensor'}, dimensions={0} | all-to-all | bytes 81920 | tf_op jit(solution)/shard_map/all_to_all | solution.py:67
  48.3 0.5 shard_map.106
  48.8 0.7 collective-permute-start.4
  49.5 0.7 collective-permute-start.5
  50.1 0.7 collective-permute-start.6
  50.8 0.7 collective-permute-start.7
  51.5 0.0 collective-permute-done.4.refs_1_.own
  51.5 0.0 collective-permute-done.5.refs_2_
  51.5 0.0 collective-permute-done.6.refs_3_
  51.5 0.0 collective-permute-done.7.refs_4_
  51.5 1.5 %shard_map.107 = bf16[4,8,640]{2,1,0:T(8,128)(2,1)S(1)} custom-call(s32[1]{0:T(128)} %bitcast.1.tensor_ref, bf16[1,8192]{1,0:T(2,128)(2,1)S(1)} %get-tuple-element.19.gain, bf16[8192,128]{1,0:T(8,128)(2,1)S(1)} %bitcast.11, bf16[8192,256]{1,0:T(8,128)(2,1)S(1)} %bitcast.7, bf16[1,128]{1,0:T(2,128)(2,1)S(1)} %get-tuple-element.20.bias, ...), custom_call_target="tpu_custom_call" | custom-call | tf_op jit(solution)/shard_map/pallas_call | solution.py:39
  53.0 8.0 %all_to_all.27.slots = bf16[4,8,640]{2,1,0:T(8,128)(2,1)S(1)} all-to-all(bf16[4,8,640]{2,1,0:T(8,128)(2,1)S(1)} %shard_map.107), channel_id=1, replica_groups=mesh['groups'=2,'tensor'=4,'section'=4] {'tensor'}, dimensions={0} | all-to-all | bytes 81920 | tf_op jit(solution)/shard_map/all_to_all | solution.py:67
  61.0 0.5 shard_map.108
  61.6 0.7 collective-permute-start.8
  62.2 0.7 collective-permute-start.9
  62.9 0.7 collective-permute-start.10
  63.6 0.7 collective-permute-start.11
  64.3 0.0 collective-permute-done.10.refs_3_
  64.3 0.0 collective-permute-done.11.refs_4_
  64.3 1.5 %shard_map.109 = bf16[4,8,640]{2,1,0:T(8,128)(2,1)S(1)} custom-call(s32[1]{0:T(128)} %bitcast.1.tensor_ref, bf16[1,8192]{1,0:T(2,128)(2,1)S(1)} %get-tuple-element.19.gain, bf16[8192,128]{1,0:T(8,128)(2,1)S(1)} %bitcast.12, bf16[8192,256]{1,0:T(8,128)(2,1)S(1)} %bitcast.8, bf16[1,128]{1,0:T(2,128)(2,1)S(1)} %get-tuple-element.20.bias, ...), custom_call_target="tpu_custom_call" | custom-call | tf_op jit(solution)/shard_map/pallas_call | solution.py:39
  65.8 8.0 %all_to_all.28.slots = bf16[4,8,640]{2,1,0:T(8,128)(2,1)S(1)} all-to-all(bf16[4,8,640]{2,1,0:T(8,128)(2,1)S(1)} %shard_map.109), channel_id=1, replica_groups=mesh['groups'=2,'tensor'=4,'section'=4] {'tensor'}, dimensions={0} | all-to-all | bytes 81920 | tf_op jit(solution)/shard_map/all_to_all | solution.py:67
  73.8 0.5 shard_map.110
  74.3 0.7 collective-permute-start.14
  75.0 0.7 collective-permute-start.13
  75.7 1.3 %collective-permute-start.12 = (bf16[2,2048]{1,0:T(2,128)(2,1)S(1)}, bf16[2,2048]{1,0:T(2,128)(2,1)S(1)}, u32[]{:S(2)}, u32[]{:S(2)}) collective-permute-start(bf16[2,2048]{1,0:T(2,128)(2,1)S(1)} %get-tuple-element.24), channel_id=1, source_target_pairs={{3,0},{7,4},{11,8},{15,12},{19,16},{23,20},{27,24},{31,28}} | collective-permute-start | bytes 24584 | tf_op jit(solution)/shard_map/ppermute | solution.py:348
  77.0 0.0 collective-permute-done.13
  77.0 16.1 %collective-permute-done.12 = bf16[2,2048]{1,0:T(2,128)(2,1)S(1)} collective-permute-done((bf16[2,2048]{1,0:T(2,128)(2,1)S(1)}, bf16[2,2048]{1,0:T(2,128)(2,1)S(1)}, u32[]{:S(2)}, u32[]{:S(2)}) %collective-permute-start.12) | collective-permute-done | bytes 8224 | tf_op jit(solution)/shard_map/ppermute | solution.py:348
  93.1 0.6 fusion.2
  (14 shorter events, 0.0 us)
Async XLA Ops:
  0.0 19.2 %copy-start.6 = (f32[1,128]{1,0:T(1,128)S(1)}, f32[1,128]{1,0:T(1,128)}, u32[]{:S(2)}) copy-start(f32[1,128]{1,0:T(1,128)} %constant.13.clone.frequency) | copy-start | bytes 1540
  0.0 19.3 %copy-start.2 = (bf16[1,8192,128]{2,1,0:T(8,128)(2,1)S(1)}, bf16[1,8192,128]{2,1,0:T(8,128)(2,1)}, u32[]{:S(2)}) copy-start(bf16[1,8192,128]{2,1,0:T(8,128)(2,1)} %param.12) | copy-start | bytes 6291460
  1.9 17.3 %all-to-all-start = ((bf16[4,176,256]{2,1,0:T(8,128)(2,1)}), bf16[4,176,256]{2,1,0:T(8,128)(2,1)S(1)}, u32[]{:S(2)}, u32[]{:S(2)}) async-start(bf16[4,176,256]{2,1,0:T(8,128)(2,1)} %shard_map.100.refs_3_), calls=%async_computation | async-start | bytes 720896 | tf_op jit(solution)/shard_map/all_to_all | solution.py:67
  9.9 1.3 %copy-start.3 = (bf16[512,2048]{1,0:T(8,128)(2,1)}, bf16[512,2048]{1,0:T(8,128)(2,1)S(1)}, u32[]{:S(2)}) copy-start(bf16[512,2048]{1,0:T(8,128)(2,1)S(1)} %get-tuple-element.16.wout) | copy-start | bytes 6291460
  19.3 2.2 %copy-start = (bf16[1,8192,256]{2,1,0:T(8,128)(2,1)S(1)}, bf16[1,8192,256]{2,1,0:T(8,128)(2,1)}, u32[]{:S(2)}) copy-start(bf16[1,8192,256]{2,1,0:T(8,128)(2,1)} %param.14) | copy-start | bytes 12582916
  21.5 9.8 %copy-start.4 = (bf16[512,2048]{1,0:T(8,128)(2,1)S(1)}, bf16[512,2048]{1,0:T(8,128)(2,1)}, u32[]{:S(2)}) copy-start(bf16[512,2048]{1,0:T(8,128)(2,1)} %copy-done.3) | copy-start | bytes 6291460
  21.5 9.8 %copy-start.5 = (bf16[8,2048]{1,0:T(8,128)(2,1)S(1)}, bf16[8,2048]{1,0:T(8,128)(2,1)}, u32[]{:S(2)}) copy-start(bf16[8,2048]{1,0:T(8,128)(2,1)} %own.1) | copy-start | bytes 98308
  21.5 17.1 %copy-start.1 = (bf16[1,8192,256]{2,1,0:T(8,128)(2,1)S(1)}, bf16[1,8192,256]{2,1,0:T(8,128)(2,1)}, u32[]{:S(2)}) copy-start(bf16[1,8192,256]{2,1,0:T(8,128)(2,1)} %param.14) | copy-start | bytes 12582916
  31.8 5.2 %collective-permute-start = (bf16[8,2048]{1,0:T(8,128)(2,1)S(1)}, bf16[8,2048]{1,0:T(8,128)(2,1)S(1)}, u32[]{:S(2)}, u32[]{:S(2)}) collective-permute-start(bf16[8,2048]{1,0:T(8,128)(2,1)S(1)} %shard_map.104), channel_id=1, source_target_pairs={{0,1},{4,5},{8,9},{12,13},{16,17},{20,21},{24,25},{28,29}} | collective-permute-start | bytes 98312 | tf_op jit(solution)/shard_map/ppermute | solution.py:58
  33.1 3.9 %collective-permute-start.1 = (bf16[8,2048]{1,0:T(8,128)(2,1)S(1)}, bf16[8,2048]{1,0:T(8,128)(2,1)S(1)}, u32[]{:S(2)}, u32[]{:S(2)}) collective-permute-start(bf16[8,2048]{1,0:T(8,128)(2,1)S(1)} %shard_map.104), channel_id=1, source_target_pairs={{0,5},{4,9},{8,13},{12,1},{16,21},{20,25},{24,29},{28,17}} | collective-permute-start | bytes 98312 | tf_op jit(solution)/shard_map/ppermute | solution.py:58
  34.4 2.9 %collective-permute-start.2 = (bf16[8,2048]{1,0:T(8,128)(2,1)S(1)}, bf16[8,2048]{1,0:T(8,128)(2,1)S(1)}, u32[]{:S(2)}, u32[]{:S(2)}) collective-permute-start(bf16[8,2048]{1,0:T(8,128)(2,1)S(1)} %shard_map.104), channel_id=1, source_target_pairs={{0,9},{4,13},{8,1},{12,5},{16,25},{20,29},{24,17},{28,21}} | collective-permute-start | bytes 98312 | tf_op jit(solution)/shard_map/ppermute | solution.py:58
  35.7 2.9 %collective-permute-start.3 = (bf16[8,2048]{1,0:T(8,128)(2,1)S(1)}, bf16[8,2048]{1,0:T(8,128)(2,1)S(1)}, u32[]{:S(2)}, u32[]{:S(2)}) collective-permute-start(bf16[8,2048]{1,0:T(8,128)(2,1)S(1)} %shard_map.104), channel_id=1, source_target_pairs={{0,13},{4,1},{8,5},{12,9},{16,29},{20,17},{24,21},{28,25}} | collective-permute-start | bytes 98312 | tf_op jit(solution)/shard_map/ppermute | solution.py:58
  48.8 2.7 %collective-permute-start.4 = (bf16[8,2048]{1,0:T(8,128)(2,1)S(1)}, bf16[8,2048]{1,0:T(8,128)(2,1)S(1)}, u32[]{:S(2)}, u32[]{:S(2)}) collective-permute-start(bf16[8,2048]{1,0:T(8,128)(2,1)S(1)} %shard_map.106), channel_id=1, source_target_pairs={{1,2},{5,6},{9,10},{13,14},{17,18},{21,22},{25,26},{29,30}} | collective-permute-start | bytes 98312 | tf_op jit(solution)/shard_map/ppermute | solution.py:58
  49.5 2.0 %collective-permute-start.5 = (bf16[8,2048]{1,0:T(8,128)(2,1)S(1)}, bf16[8,2048]{1,0:T(8,128)(2,1)S(1)}, u32[]{:S(2)}, u32[]{:S(2)}) collective-permute-start(bf16[8,2048]{1,0:T(8,128)(2,1)S(1)} %shard_map.106), channel_id=1, source_target_pairs={{1,6},{5,10},{9,14},{13,2},{17,22},{21,26},{25,30},{29,18}} | collective-permute-start | bytes 98312 | tf_op jit(solution)/shard_map/ppermute | solution.py:58
  50.1 1.4 %collective-permute-start.6 = (bf16[8,2048]{1,0:T(8,128)(2,1)S(1)}, bf16[8,2048]{1,0:T(8,128)(2,1)S(1)}, u32[]{:S(2)}, u32[]{:S(2)}) collective-permute-start(bf16[8,2048]{1,0:T(8,128)(2,1)S(1)} %shard_map.106), channel_id=1, source_target_pairs={{1,10},{5,14},{9,2},{13,6},{17,26},{21,30},{25,18},{29,22}} | collective-permute-start | bytes 98312 | tf_op jit(solution)/shard_map/ppermute | solution.py:58
  50.8 0.7 collective-permute-start.7
  61.6 2.7 %collective-permute-start.8 = (bf16[8,2048]{1,0:T(8,128)(2,1)S(1)}, bf16[8,2048]{1,0:T(8,128)(2,1)S(1)}, u32[]{:S(2)}, u32[]{:S(2)}) collective-permute-start(bf16[8,2048]{1,0:T(8,128)(2,1)S(1)} %shard_map.108), channel_id=1, source_target_pairs={{2,3},{6,7},{10,11},{14,15},{18,19},{22,23},{26,27},{30,31}} | collective-permute-start | bytes 98312 | tf_op jit(solution)/shard_map/ppermute | solution.py:58
  62.2 2.0 %collective-permute-start.9 = (bf16[8,2048]{1,0:T(8,128)(2,1)S(1)}, bf16[8,2048]{1,0:T(8,128)(2,1)S(1)}, u32[]{:S(2)}, u32[]{:S(2)}) collective-permute-start(bf16[8,2048]{1,0:T(8,128)(2,1)S(1)} %shard_map.108), channel_id=1, source_target_pairs={{2,7},{6,11},{10,15},{14,3},{18,23},{22,27},{26,31},{30,19}} | collective-permute-start | bytes 98312 | tf_op jit(solution)/shard_map/ppermute | solution.py:58
  62.9 1.4 %collective-permute-start.10 = (bf16[8,2048]{1,0:T(8,128)(2,1)S(1)}, bf16[8,2048]{1,0:T(8,128)(2,1)S(1)}, u32[]{:S(2)}, u32[]{:S(2)}) collective-permute-start(bf16[8,2048]{1,0:T(8,128)(2,1)S(1)} %shard_map.108), channel_id=1, source_target_pairs={{2,11},{6,15},{10,3},{14,7},{18,27},{22,31},{26,19},{30,23}} | collective-permute-start | bytes 98312 | tf_op jit(solution)/shard_map/ppermute | solution.py:58
  63.6 0.7 collective-permute-start.11
  74.3 2.7 %collective-permute-start.14 = (bf16[2,2048]{1,0:T(2,128)(2,1)S(1)}, bf16[2,2048]{1,0:T(2,128)(2,1)S(1)}, u32[]{:S(2)}, u32[]{:S(2)}) collective-permute-start(bf16[2,2048]{1,0:T(2,128)(2,1)S(1)} %get-tuple-element.26), channel_id=1, source_target_pairs={{3,2},{7,6},{11,10},{15,14},{19,18},{23,22},{27,26},{31,30}} | collective-permute-start | bytes 24584 | tf_op jit(solution)/shard_map/ppermute | solution.py:348
  75.0 2.0 %collective-permute-start.13 = (bf16[2,2048]{1,0:T(2,128)(2,1)S(1)}, bf16[2,2048]{1,0:T(2,128)(2,1)S(1)}, u32[]{:S(2)}, u32[]{:S(2)}) collective-permute-start(bf16[2,2048]{1,0:T(2,128)(2,1)S(1)} %get-tuple-element.25), channel_id=1, source_target_pairs={{3,1},{7,5},{11,9},{15,13},{19,17},{23,21},{27,25},{31,29}} | collective-permute-start | bytes 24584 | tf_op jit(solution)/shard_map/ppermute | solution.py:348
  75.7 17.4 %collective-permute-start.12 = (bf16[2,2048]{1,0:T(2,128)(2,1)S(1)}, bf16[2,2048]{1,0:T(2,128)(2,1)S(1)}, u32[]{:S(2)}, u32[]{:S(2)}) collective-permute-start(bf16[2,2048]{1,0:T(2,128)(2,1)S(1)} %get-tuple-element.24), channel_id=1, source_target_pairs={{3,0},{7,4},{11,8},{15,12},{19,16},{23,20},{27,24},{31,28}} | collective-permute-start | bytes 24584 | tf_op jit(solution)/shard_map/ppermute | solution.py:348

commit v4 on v3

--- a/solution.py
+++ b/solution.py
@@ -51,6 +51,8 @@
         self.count = lax.axis_size("tensor")
         self.sections = lax.axis_size("section")
         self.direct = self.count <= DIRECT_PEERS
+        far = sorted(range(1, self.count), key=lambda step: -max(step, self.count - step))
+        self.steps = tuple(far) + (0,)
 
     def send(self, value, origin, target, step):
         n, m = self.count, self.sections
@@ -59,7 +61,7 @@
 
     def advance(self, value, origin, target):
         if self.direct:
-            return [self.send(value, origin, target, step) for step in range(self.count)]
+            return [self.send(value, origin, target, step) for step in self.steps]
         value = lax.ppermute(value, "section", [(origin, target)])
         return [lax.all_gather(value, "tensor", axis=1, tiled=True)]
 
@@ -152,14 +154,14 @@
 
 
 def project_kernel(info, tensor_ref, gain, wq, wkv, bias, counts, cosine, sine, *refs):
-    n, heads_dev, group, tokens, width, rotated_order = info
+    n, heads_dev, group, tokens, width, steps = info
     packs, *pieces, out = refs
     features = gain.shape[1]
     slice_len = features // n
-    if rotated_order:
+    if steps:
         wide = [piece[...].astype(jnp.float32) for piece in pieces]
         me = tensor_ref[0]
-        starts = [pl.multiple_of((me + n - k) % n * slice_len, HD) for k in range(n)]
+        starts = [pl.multiple_of((me + n - step) % n * slice_len, HD) for step in steps]
     else:
         starts = [k * slice_len for k in range(n)]
         wide = [pieces[0][:, at : at + slice_len].astype(jnp.float32) for at in starts]
@@ -322,9 +324,10 @@
     project_info = (n, heads_dev, group, tokens, width)
     pieces = [first]
     own = hidden
+    order = ()
     for layer in range(sections):
         sent = kernel_call(
-            functools.partial(project_kernel, project_info + (ring.direct and layer > 0,)),
+            functools.partial(project_kernel, project_info + (order,)),
             [jax.ShapeDtypeStruct((n, rows, message), bf16)],
             [SMEM] + [VMEM] * (8 + len(pieces)),
             many=False,
@@ -341,7 +344,8 @@
         )(own, wout, cosine, sine, parts)
         if layer < sections - 1:
             pieces = ring.advance(stream[0], layer, layer + 1)
-            own = pieces[0] if ring.direct else own_slice(pieces[0], tensor_id, slice_len)
+            order = ring.steps if ring.direct else ()
+            own = pieces[-1] if ring.direct else own_slice(pieces[0], tensor_id, slice_len)
     last = sections - 1
     result = jnp.where(section_id == last, stream[last], jnp.zeros_like(stream[last]))
     for target in range(last):

time: 94.3 us -> 92.9 us (0.985)
  waiting for transfers between devices: 25.7 us -> 24.3 us
    ppermute x3, waiting for transfers between devices: 16.1 us -> 14.7 us  [shards(): result = result + lax.ppermute(stream[target], 'section', [(last, target)])]
where the time goes in v4:
time: 92.9 us; the launch traced here: 92.3 us
  blocking collectives  32.7 us (35%)
  waiting for transfers between devices  24.3 us (26%)
  starting transfers between devices  19.5 us (21%)
  Pallas kernels  11.5 us (12%)
  local copies, waits for them, and re-layouts  3.52 us (4%)
    all_to_all x4, blocking collectives, trade(): lax.all_to_all(values, 'tensor', split_axis=0, concat_axis=0, tiled=True)  32.7 us
    ppermute x3, waiting for transfers between devices, shards(): result = result + lax.ppermute(stream[target], 'section', [(last, target)])  14.7 us
    ppermute x12, starting transfers between devices, send(): return lax.ppermute(value, ('tensor', 'section'), perm)  10.5 us
    all_to_all x1, waiting for transfers between devices, trade(): lax.all_to_all(values, 'tensor', split_axis=0, concat_axis=0, tiled=True)  8.02 us
    pallas_call x9, Pallas kernels, placed(): call(*[put(value, pltpu.VMEM) if spec is VMEM else value for value, spec...  7.97 us
    all_to_all x1, starting transfers between devices, trade(): lax.all_to_all(values, 'tensor', split_axis=0, concat_axis=0, tiled=True)  6.35 us
    unnamed x14, local copies, waits for them, and re-layouts  3.52 us
    ppermute x3, starting transfers between devices, shards(): result = result + lax.ppermute(stream[target], 'section', [(last, target)])  2.63 us
  transfers between devices with their start and end apart: 16, of which 4 were waited for; matrix products, arithmetic and copies ran while one was open for 0% of the time, Pallas kernels for 2%

profile of v4, /device:TPU:0, one launch (start us, length us, event | category | flops | bytes accessed | tf_op | source)
XLA Modules:
  0.0 92.3 jit_solution(13771893267097314999)
XLA Ops:
  0.0 1.9 %shard_map.100.refs_3_ = bf16[4,176,256]{2,1,0:T(8,128)(2,1)} custom-call(s32[1]{0:T(128)} %bitcast.1.tensor_ref, s32[2,4]{1,0:T(2,128)} %table.1, s32[2]{0:T(128)} %context.1, bf16[96,1024]{1,0:T(8,128)(2,1)} %bitcast.14, bf16[8,2048]{1,0:T(8,128)(2,1)} %own.1), custom_call_target="tpu_custom_call" | custom-call | tf_op jit(solution)/shard_map/pallas_call | solution.py:38
  1.9 6.3 %all-to-all-start = ((bf16[4,176,256]{2,1,0:T(8,128)(2,1)}), bf16[4,176,256]{2,1,0:T(8,128)(2,1)S(1)}, u32[]{:S(2)}, u32[]{:S(2)}) async-start(bf16[4,176,256]{2,1,0:T(8,128)(2,1)} %shard_map.100.refs_3_), calls=%async_computation | async-start | bytes 720896 | tf_op jit(solution)/shard_map/all_to_all | solution.py:69
  8.2 1.6 %shard_map.101 = (bf16[512,2048]{1,0:T(8,128)(2,1)S(1)}, bf16[1,8192]{1,0:T(2,128)(2,1)S(1)}, bf16[1,128]{1,0:T(2,128)(2,1)S(1)}) custom-call(bf16[512,2048]{1,0:T(8,128)(2,1)} %bitcast.13, bf16[1,8192]{1,0:T(2,128)(2,1)} %refs_1_.1, bf16[1,128]{1,0:T(2,128)(2,1)} %refs_2_.1, bf16[4,176,256]{2,1,0:T(8,128)(2,1)} %shard_map.100.refs_3_), custom_call_target="tpu_custom_call" | custom-call | tf_op jit(solution)/shard_map/pallas_call | solution.py:86
  9.9 1.3 %copy-done.3 = bf16[512,2048]{1,0:T(8,128)(2,1)} copy-done((bf16[512,2048]{1,0:T(8,128)(2,1)}, bf16[512,2048]{1,0:T(8,128)(2,1)S(1)}, u32[]{:S(2)}) %copy-start.3) | copy-done | bytes 2097176
  11.2 8.0 %all-to-all-done.packs.refs_0_ = bf16[4,176,256]{2,1,0:T(8,128)(2,1)S(1)} async-done(((bf16[4,176,256]{2,1,0:T(8,128)(2,1)}), bf16[4,176,256]{2,1,0:T(8,128)(2,1)S(1)}, u32[]{:S(2)}, u32[]{:S(2)}) %all-to-all-start) | async-done | bytes 360480 | tf_op jit(solution)/shard_map/all_to_all | solution.py:69
  19.2 0.1 shard_map.102
  19.3 0.0 copy-start
  19.3 2.2 %copy-done = bf16[1,8192,256]{2,1,0:T(8,128)(2,1)S(1)} copy-done((bf16[1,8192,256]{2,1,0:T(8,128)(2,1)S(1)}, bf16[1,8192,256]{2,1,0:T(8,128)(2,1)}, u32[]{:S(2)}) %copy-start) | copy-done | bytes 4194328
  21.5 1.4 %shard_map.103 = bf16[4,8,640]{2,1,0:T(8,128)(2,1)S(1)} custom-call(s32[1]{0:T(128)} %bitcast.1.tensor_ref, bf16[1,8192]{1,0:T(2,128)(2,1)S(1)} %get-tuple-element.19.gain, bf16[8192,128]{1,0:T(8,128)(2,1)S(1)} %bitcast.9, bf16[8192,256]{1,0:T(8,128)(2,1)S(1)} %bitcast.5, bf16[1,128]{1,0:T(2,128)(2,1)S(1)} %get-tuple-element.20.bias, ...), custom_call_target="tpu_custom_call" | custom-call | tf_op jit(solution)/shard_map/pallas_call | solution.py:39
  22.9 8.3 %all_to_all.25.slots = bf16[4,8,640]{2,1,0:T(8,128)(2,1)S(1)} all-to-all(bf16[4,8,640]{2,1,0:T(8,128)(2,1)S(1)} %shard_map.103), channel_id=1, replica_groups=mesh['groups'=2,'tensor'=4,'section'=4] {'tensor'}, dimensions={0} | all-to-all | bytes 81920 | tf_op jit(solution)/shard_map/all_to_all | solution.py:69
  31.3 0.5 shard_map.104
  31.8 1.3 %collective-permute-start = (bf16[8,2048]{1,0:T(8,128)(2,1)S(1)}, bf16[8,2048]{1,0:T(8,128)(2,1)S(1)}, u32[]{:S(2)}, u32[]{:S(2)}) collective-permute-start(bf16[8,2048]{1,0:T(8,128)(2,1)S(1)} %shard_map.104), channel_id=1, source_target_pairs={{0,1},{4,5},{8,9},{12,13},{16,17},{20,21},{24,25},{28,29}} | collective-permute-start | bytes 98312 | tf_op jit(solution)/shard_map/ppermute | solution.py:60
  33.1 1.3 %collective-permute-start.1 = (bf16[8,2048]{1,0:T(8,128)(2,1)S(1)}, bf16[8,2048]{1,0:T(8,128)(2,1)S(1)}, u32[]{:S(2)}, u32[]{:S(2)}) collective-permute-start(bf16[8,2048]{1,0:T(8,128)(2,1)S(1)} %shard_map.104), channel_id=1, source_target_pairs={{0,5},{4,9},{8,13},{12,1},{16,21},{20,25},{24,29},{28,17}} | collective-permute-start | bytes 98312 | tf_op jit(solution)/shard_map/ppermute | solution.py:60
  34.4 1.3 %collective-permute-start.2 = (bf16[8,2048]{1,0:T(8,128)(2,1)S(1)}, bf16[8,2048]{1,0:T(8,128)(2,1)S(1)}, u32[]{:S(2)}, u32[]{:S(2)}) collective-permute-start(bf16[8,2048]{1,0:T(8,128)(2,1)S(1)} %shard_map.104), channel_id=1, source_target_pairs={{0,13},{4,1},{8,5},{12,9},{16,29},{20,17},{24,21},{28,25}} | collective-permute-start | bytes 98312 | tf_op jit(solution)/shard_map/ppermute | solution.py:60
  35.7 1.3 %collective-permute-start.3 = (bf16[8,2048]{1,0:T(8,128)(2,1)S(1)}, bf16[8,2048]{1,0:T(8,128)(2,1)S(1)}, u32[]{:S(2)}, u32[]{:S(2)}) collective-permute-start(bf16[8,2048]{1,0:T(8,128)(2,1)S(1)} %shard_map.104), channel_id=1, source_target_pairs={{0,9},{4,13},{8,1},{12,5},{16,25},{20,29},{24,17},{28,21}} | collective-permute-start | bytes 98312 | tf_op jit(solution)/shard_map/ppermute | solution.py:60
  37.0 0.0 collective-permute-done.refs_4_.own
  37.0 0.0 collective-permute-done.1.refs_1_
  37.0 0.3 collective-permute-done.2.refs_2_
  37.3 1.3 %collective-permute-done.3.refs_3_ = bf16[8,2048]{1,0:T(8,128)(2,1)S(1)} collective-permute-done((bf16[8,2048]{1,0:T(8,128)(2,1)S(1)}, bf16[8,2048]{1,0:T(8,128)(2,1)S(1)}, u32[]{:S(2)}, u32[]{:S(2)}) %collective-permute-start.3) | collective-permute-done | bytes 32800 | tf_op jit(solution)/shard_map/ppermute | solution.py:60
  38.6 1.5 %shard_map.105 = bf16[4,8,640]{2,1,0:T(8,128)(2,1)S(1)} custom-call(s32[1]{0:T(128)} %bitcast.1.tensor_ref, bf16[1,8192]{1,0:T(2,128)(2,1)S(1)} %get-tuple-element.19.gain, bf16[8192,128]{1,0:T(8,128)(2,1)S(1)} %bitcast.10, bf16[8192,256]{1,0:T(8,128)(2,1)S(1)} %bitcast.6, bf16[1,128]{1,0:T(2,128)(2,1)S(1)} %get-tuple-element.20.bias, ...), custom_call_target="tpu_custom_call" | custom-call | tf_op jit(solution)/shard_map/pallas_call | solution.py:39
  40.1 8.2 %all_to_all.26.slots = bf16[4,8,640]{2,1,0:T(8,128)(2,1)S(1)} all-to-all(bf16[4,8,640]{2,1,0:T(8,128)(2,1)S(1)} %shard_map.105), channel_id=1, replica_groups=mesh['groups'=2,'tensor'=4,'section'=4] {'tensor'}, dimensions={0} | all-to-all | bytes 81920 | tf_op jit(solution)/shard_map/all_to_all | solution.py:69
  48.3 0.5 shard_map.106
  48.8 0.7 collective-permute-start.4
  49.5 0.7 collective-permute-start.5
  50.1 0.7 collective-permute-start.6
  50.8 0.7 collective-permute-start.7
  51.5 0.0 collective-permute-done.4.refs_4_.own
  51.5 0.0 collective-permute-done.5.refs_1_
  51.5 0.0 collective-permute-done.7.refs_3_
  51.5 1.5 %shard_map.107 = bf16[4,8,640]{2,1,0:T(8,128)(2,1)S(1)} custom-call(s32[1]{0:T(128)} %bitcast.1.tensor_ref, bf16[1,8192]{1,0:T(2,128)(2,1)S(1)} %get-tuple-element.19.gain, bf16[8192,128]{1,0:T(8,128)(2,1)S(1)} %bitcast.11, bf16[8192,256]{1,0:T(8,128)(2,1)S(1)} %bitcast.7, bf16[1,128]{1,0:T(2,128)(2,1)S(1)} %get-tuple-element.20.bias, ...), custom_call_target="tpu_custom_call" | custom-call | tf_op jit(solution)/shard_map/pallas_call | solution.py:39
  53.0 8.0 %all_to_all.27.slots = bf16[4,8,640]{2,1,0:T(8,128)(2,1)S(1)} all-to-all(bf16[4,8,640]{2,1,0:T(8,128)(2,1)S(1)} %shard_map.107), channel_id=1, replica_groups=mesh['groups'=2,'tensor'=4,'section'=4] {'tensor'}, dimensions={0} | all-to-all | bytes 81920 | tf_op jit(solution)/shard_map/all_to_all | solution.py:69
  61.0 0.5 shard_map.108
  61.6 0.7 collective-permute-start.8
  62.2 0.7 collective-permute-start.9
  62.9 0.7 collective-permute-start.10
  63.6 0.7 collective-permute-start.11
  64.3 0.0 collective-permute-done.8.refs_4_.own
  64.3 0.0 collective-permute-done.10.refs_2_
  64.3 0.0 collective-permute-done.11.refs_3_
  64.3 1.5 %shard_map.109 = bf16[4,8,640]{2,1,0:T(8,128)(2,1)S(1)} custom-call(s32[1]{0:T(128)} %bitcast.1.tensor_ref, bf16[1,8192]{1,0:T(2,128)(2,1)S(1)} %get-tuple-element.19.gain, bf16[8192,128]{1,0:T(8,128)(2,1)S(1)} %bitcast.12, bf16[8192,256]{1,0:T(8,128)(2,1)S(1)} %bitcast.8, bf16[1,128]{1,0:T(2,128)(2,1)S(1)} %get-tuple-element.20.bias, ...), custom_call_target="tpu_custom_call" | custom-call | tf_op jit(solution)/shard_map/pallas_call | solution.py:39
  65.8 8.1 %all_to_all.28.slots = bf16[4,8,640]{2,1,0:T(8,128)(2,1)S(1)} all-to-all(bf16[4,8,640]{2,1,0:T(8,128)(2,1)S(1)} %shard_map.109), channel_id=1, replica_groups=mesh['groups'=2,'tensor'=4,'section'=4] {'tensor'}, dimensions={0} | all-to-all | bytes 81920 | tf_op jit(solution)/shard_map/all_to_all | solution.py:69
  73.8 0.5 shard_map.110
  74.3 0.7 collective-permute-start.14
  75.0 0.7 collective-permute-start.13
  75.7 1.3 %collective-permute-start.12 = (bf16[2,2048]{1,0:T(2,128)(2,1)S(1)}, bf16[2,2048]{1,0:T(2,128)(2,1)S(1)}, u32[]{:S(2)}, u32[]{:S(2)}) collective-permute-start(bf16[2,2048]{1,0:T(2,128)(2,1)S(1)} %get-tuple-element.24), channel_id=1, source_target_pairs={{3,0},{7,4},{11,8},{15,12},{19,16},{23,20},{27,24},{31,28}} | collective-permute-start | bytes 24584 | tf_op jit(solution)/shard_map/ppermute | solution.py:352
  77.0 0.0 collective-permute-done.13
  77.0 14.7 %collective-permute-done.12 = bf16[2,2048]{1,0:T(2,128)(2,1)S(1)} collective-permute-done((bf16[2,2048]{1,0:T(2,128)(2,1)S(1)}, bf16[2,2048]{1,0:T(2,128)(2,1)S(1)}, u32[]{:S(2)}, u32[]{:S(2)}) %collective-permute-start.12) | collective-permute-done | bytes 8224 | tf_op jit(solution)/shard_map/ppermute | solution.py:352
  91.7 0.6 fusion.2
  (14 shorter events, 0.0 us)
Async XLA Ops:
  0.0 19.2 %copy-start.6 = (f32[1,128]{1,0:T(1,128)S(1)}, f32[1,128]{1,0:T(1,128)}, u32[]{:S(2)}) copy-start(f32[1,128]{1,0:T(1,128)} %constant.13.clone.frequency) | copy-start | bytes 1540
  0.0 19.3 %copy-start.2 = (bf16[1,8192,128]{2,1,0:T(8,128)(2,1)S(1)}, bf16[1,8192,128]{2,1,0:T(8,128)(2,1)}, u32[]{:S(2)}) copy-start(bf16[1,8192,128]{2,1,0:T(8,128)(2,1)} %param.12) | copy-start | bytes 6291460
  1.9 17.3 %all-to-all-start = ((bf16[4,176,256]{2,1,0:T(8,128)(2,1)}), bf16[4,176,256]{2,1,0:T(8,128)(2,1)S(1)}, u32[]{:S(2)}, u32[]{:S(2)}) async-start(bf16[4,176,256]{2,1,0:T(8,128)(2,1)} %shard_map.100.refs_3_), calls=%async_computation | async-start | bytes 720896 | tf_op jit(solution)/shard_map/all_to_all | solution.py:69
  9.9 1.3 %copy-start.3 = (bf16[512,2048]{1,0:T(8,128)(2,1)}, bf16[512,2048]{1,0:T(8,128)(2,1)S(1)}, u32[]{:S(2)}) copy-start(bf16[512,2048]{1,0:T(8,128)(2,1)S(1)} %get-tuple-element.16.wout) | copy-start | bytes 6291460
  19.3 2.2 %copy-start = (bf16[1,8192,256]{2,1,0:T(8,128)(2,1)S(1)}, bf16[1,8192,256]{2,1,0:T(8,128)(2,1)}, u32[]{:S(2)}) copy-start(bf16[1,8192,256]{2,1,0:T(8,128)(2,1)} %param.14) | copy-start | bytes 12582916
  21.5 9.8 %copy-start.4 = (bf16[512,2048]{1,0:T(8,128)(2,1)S(1)}, bf16[512,2048]{1,0:T(8,128)(2,1)}, u32[]{:S(2)}) copy-start(bf16[512,2048]{1,0:T(8,128)(2,1)} %copy-done.3) | copy-start | bytes 6291460
  21.5 9.8 %copy-start.5 = (bf16[8,2048]{1,0:T(8,128)(2,1)S(1)}, bf16[8,2048]{1,0:T(8,128)(2,1)}, u32[]{:S(2)}) copy-start(bf16[8,2048]{1,0:T(8,128)(2,1)} %own.1) | copy-start | bytes 98308
  21.5 17.1 %copy-start.1 = (bf16[1,8192,256]{2,1,0:T(8,128)(2,1)S(1)}, bf16[1,8192,256]{2,1,0:T(8,128)(2,1)}, u32[]{:S(2)}) copy-start(bf16[1,8192,256]{2,1,0:T(8,128)(2,1)} %param.14) | copy-start | bytes 12582916
  31.8 5.2 %collective-permute-start = (bf16[8,2048]{1,0:T(8,128)(2,1)S(1)}, bf16[8,2048]{1,0:T(8,128)(2,1)S(1)}, u32[]{:S(2)}, u32[]{:S(2)}) collective-permute-start(bf16[8,2048]{1,0:T(8,128)(2,1)S(1)} %shard_map.104), channel_id=1, source_target_pairs={{0,1},{4,5},{8,9},{12,13},{16,17},{20,21},{24,25},{28,29}} | collective-permute-start | bytes 98312 | tf_op jit(solution)/shard_map/ppermute | solution.py:60
  33.1 3.9 %collective-permute-start.1 = (bf16[8,2048]{1,0:T(8,128)(2,1)S(1)}, bf16[8,2048]{1,0:T(8,128)(2,1)S(1)}, u32[]{:S(2)}, u32[]{:S(2)}) collective-permute-start(bf16[8,2048]{1,0:T(8,128)(2,1)S(1)} %shard_map.104), channel_id=1, source_target_pairs={{0,5},{4,9},{8,13},{12,1},{16,21},{20,25},{24,29},{28,17}} | collective-permute-start | bytes 98312 | tf_op jit(solution)/shard_map/ppermute | solution.py:60
  34.4 2.9 %collective-permute-start.2 = (bf16[8,2048]{1,0:T(8,128)(2,1)S(1)}, bf16[8,2048]{1,0:T(8,128)(2,1)S(1)}, u32[]{:S(2)}, u32[]{:S(2)}) collective-permute-start(bf16[8,2048]{1,0:T(8,128)(2,1)S(1)} %shard_map.104), channel_id=1, source_target_pairs={{0,13},{4,1},{8,5},{12,9},{16,29},{20,17},{24,21},{28,25}} | collective-permute-start | bytes 98312 | tf_op jit(solution)/shard_map/ppermute | solution.py:60
  35.7 2.9 %collective-permute-start.3 = (bf16[8,2048]{1,0:T(8,128)(2,1)S(1)}, bf16[8,2048]{1,0:T(8,128)(2,1)S(1)}, u32[]{:S(2)}, u32[]{:S(2)}) collective-permute-start(bf16[8,2048]{1,0:T(8,128)(2,1)S(1)} %shard_map.104), channel_id=1, source_target_pairs={{0,9},{4,13},{8,1},{12,5},{16,25},{20,29},{24,17},{28,21}} | collective-permute-start | bytes 98312 | tf_op jit(solution)/shard_map/ppermute | solution.py:60
  48.8 2.7 %collective-permute-start.4 = (bf16[8,2048]{1,0:T(8,128)(2,1)S(1)}, bf16[8,2048]{1,0:T(8,128)(2,1)S(1)}, u32[]{:S(2)}, u32[]{:S(2)}) collective-permute-start(bf16[8,2048]{1,0:T(8,128)(2,1)S(1)} %shard_map.106), channel_id=1, source_target_pairs={{1,2},{5,6},{9,10},{13,14},{17,18},{21,22},{25,26},{29,30}} | collective-permute-start | bytes 98312 | tf_op jit(solution)/shard_map/ppermute | solution.py:60
  49.5 2.0 %collective-permute-start.5 = (bf16[8,2048]{1,0:T(8,128)(2,1)S(1)}, bf16[8,2048]{1,0:T(8,128)(2,1)S(1)}, u32[]{:S(2)}, u32[]{:S(2)}) collective-permute-start(bf16[8,2048]{1,0:T(8,128)(2,1)S(1)} %shard_map.106), channel_id=1, source_target_pairs={{1,6},{5,10},{9,14},{13,2},{17,22},{21,26},{25,30},{29,18}} | collective-permute-start | bytes 98312 | tf_op jit(solution)/shard_map/ppermute | solution.py:60
  50.1 1.4 %collective-permute-start.6 = (bf16[8,2048]{1,0:T(8,128)(2,1)S(1)}, bf16[8,2048]{1,0:T(8,128)(2,1)S(1)}, u32[]{:S(2)}, u32[]{:S(2)}) collective-permute-start(bf16[8,2048]{1,0:T(8,128)(2,1)S(1)} %shard_map.106), channel_id=1, source_target_pairs={{1,14},{5,2},{9,6},{13,10},{17,30},{21,18},{25,22},{29,26}} | collective-permute-start | bytes 98312 | tf_op jit(solution)/shard_map/ppermute | solution.py:60
  50.8 0.7 collective-permute-start.7
  61.6 2.7 %collective-permute-start.8 = (bf16[8,2048]{1,0:T(8,128)(2,1)S(1)}, bf16[8,2048]{1,0:T(8,128)(2,1)S(1)}, u32[]{:S(2)}, u32[]{:S(2)}) collective-permute-start(bf16[8,2048]{1,0:T(8,128)(2,1)S(1)} %shard_map.108), channel_id=1, source_target_pairs={{2,3},{6,7},{10,11},{14,15},{18,19},{22,23},{26,27},{30,31}} | collective-permute-start | bytes 98312 | tf_op jit(solution)/shard_map/ppermute | solution.py:60
  62.2 2.0 %collective-permute-start.9 = (bf16[8,2048]{1,0:T(8,128)(2,1)S(1)}, bf16[8,2048]{1,0:T(8,128)(2,1)S(1)}, u32[]{:S(2)}, u32[]{:S(2)}) collective-permute-start(bf16[8,2048]{1,0:T(8,128)(2,1)S(1)} %shard_map.108), channel_id=1, source_target_pairs={{2,7},{6,11},{10,15},{14,3},{18,23},{22,27},{26,31},{30,19}} | collective-permute-start | bytes 98312 | tf_op jit(solution)/shard_map/ppermute | solution.py:60
  62.9 1.4 %collective-permute-start.10 = (bf16[8,2048]{1,0:T(8,128)(2,1)S(1)}, bf16[8,2048]{1,0:T(8,128)(2,1)S(1)}, u32[]{:S(2)}, u32[]{:S(2)}) collective-permute-start(bf16[8,2048]{1,0:T(8,128)(2,1)S(1)} %shard_map.108), channel_id=1, source_target_pairs={{2,15},{6,3},{10,7},{14,11},{18,31},{22,19},{26,23},{30,27}} | collective-permute-start | bytes 98312 | tf_op jit(solution)/shard_map/ppermute | solution.py:60
  63.6 0.7 collective-permute-start.11
  74.3 2.7 %collective-permute-start.14 = (bf16[2,2048]{1,0:T(2,128)(2,1)S(1)}, bf16[2,2048]{1,0:T(2,128)(2,1)S(1)}, u32[]{:S(2)}, u32[]{:S(2)}) collective-permute-start(bf16[2,2048]{1,0:T(2,128)(2,1)S(1)} %get-tuple-element.26), channel_id=1, source_target_pairs={{3,2},{7,6},{11,10},{15,14},{19,18},{23,22},{27,26},{31,30}} | collective-permute-start | bytes 24584 | tf_op jit(solution)/shard_map/ppermute | solution.py:352
  75.0 2.0 %collective-permute-start.13 = (bf16[2,2048]{1,0:T(2,128)(2,1)S(1)}, bf16[2,2048]{1,0:T(2,128)(2,1)S(1)}, u32[]{:S(2)}, u32[]{:S(2)}) collective-permute-start(bf16[2,2048]{1,0:T(2,128)(2,1)S(1)} %get-tuple-element.25), channel_id=1, source_target_pairs={{3,1},{7,5},{11,9},{15,13},{19,17},{23,21},{27,25},{31,29}} | collective-permute-start | bytes 24584 | tf_op jit(solution)/shard_map/ppermute | solution.py:352
  75.7 16.0 %collective-permute-start.12 = (bf16[2,2048]{1,0:T(2,128)(2,1)S(1)}, bf16[2,2048]{1,0:T(2,128)(2,1)S(1)}, u32[]{:S(2)}, u32[]{:S(2)}) collective-permute-start(bf16[2,2048]{1,0:T(2,128)(2,1)S(1)} %get-tuple-element.24), channel_id=1, source_target_pairs={{3,0},{7,4},{11,8},{15,12},{19,16},{23,20},{27,24},{31,28}} | collective-permute-start | bytes 24584 | tf_op jit(solution)/shard_map/ppermute | solution.py:352
